TPU v7x, 512 devices: a whole 4x4x16 slice. The times are simulated.
512 devices in a mesh: users: 32 (over y, x, core), camps: 16 (over z).
Axes of the slice: x: 4, y: 4, z: 16, core: 2. Of those that a mesh axis runs over, the one named last changes fastest.
Arguments:
- scores: bfloat16 [64, 16, 12, 128, 128], P('users', 'camps'), may hold values from -12 to 12
- elig_ids: int32 [64, 16, 12], P('users', 'camps'), may hold values from 0 to 63, as said below
- elig_counts: int32 [64, 16], P('users', 'camps'), may hold values from 1 to 12, as said below
- activity: bfloat16 [24, 8192], P(None, 'users'), may hold values from 0.019897461 to 0.19921875
- prices: float32 [24, 131072], P(None, ('users', 'camps')), may hold values from 0 to 1.5
- spend_limit: float32 [24, 131072], P(None, ('users', 'camps')), may hold values from 3.072 to 16.896
Outputs:
- new_prices: float32 [24, 131072], P(None, ('users', 'camps'))
- direction: float32 [24, 131072], P(None, ('users', 'camps'))
Inputs may be any that keep to these rules, and one draw needn't show every extreme that they name: `elig_ids`: the 12 numbers of each list are all different. `elig_counts`: in every campaign group some user block has 12 eligible slots.
All inputs are finite; a program needn't handle non-finite values.
Results may differ from a plain program's by a relative error of at most 0.008.
Values may be sent and summed in bfloat16 or wider, within the bound.
No kernel may reach another device: no remote copies, remote signals or barrier semaphores. Data moves between devices by JAX's collectives and lax.ppermute only.
A program may use at most 64 MiB of HBM per device.

v0:
```python
import functools

import jax
import jax.numpy as jnp
from jax import lax
from jax.sharding import Mesh
from jax.sharding import PartitionSpec as P

STEPS = 2
USERS = ("users_0", "users_1", "users_2")
USERS_CAMPS = ("users_0", "users_1", "users_2", "camps")


def sent_to_all(value, axis):
    copies = jnp.broadcast_to(value, (lax.axis_size(axis), *value.shape))
    return lax.all_to_all(copies, axis, split_axis=0, concat_axis=0, tiled=True)


def in_order(parts, dim):
    dims = list(parts.shape[1:])
    dims[dim] *= parts.shape[0]
    return jnp.moveaxis(parts, 0, dim).reshape(dims)


def gathered_copies(value, axis, dim):
    parts = sent_to_all(value, axis)
    return in_order(parts, dim)


def cut_along(value, dim, count):
    before, after = (value.shape[:dim], value.shape[dim + 1 :])
    return jnp.moveaxis(value.reshape(*before, count, -1, *after), dim, 0)


def sum_at_owner(value, axis, dim):
    parts = cut_along(value, dim, lax.axis_size(axis))
    arrived = lax.all_to_all(parts, axis, split_axis=0, concat_axis=0, tiled=True)
    return arrived.sum(axis=0)


def over_axes(value, axes):
    return functools.reduce(lax.psum, axes, value)


def local_usage(group_bf, scores, elig_ids, elig_counts, activity):
    hours = activity.shape[0]
    tile = scores.shape[-1]
    blocks = scores.shape[0]
    slots = scores.shape[2]
    camp_blocks = group_bf.shape[1] // tile
    table = group_bf.reshape(hours, camp_blocks, tile)
    acts = activity.reshape(hours, blocks, tile)
    tiles = scores[:, 0]
    id_rows = elig_ids[:, 0]
    count_rows = elig_counts[:, 0]
    columns = jnp.arange(camp_blocks, dtype=jnp.int32)
    init = jnp.zeros((hours, camp_blocks, tile), jnp.float32)
    slot_ids = jnp.arange(slots, dtype=jnp.int32)

    def one_block(total, inputs):
        act_b, tile_b, ids_b, count_b = inputs
        picked = jnp.take(table, ids_b, axis=1)
        cost = jnp.einsum("hu,hkt->kut", act_b, picked, preferred_element_type=jnp.float32)
        live = (slot_ids < count_b).astype(jnp.float32)
        share = (
            jnp.clip(0.5 + (tile_b.astype(jnp.float32) - cost) / 2.0, 0.0, 1.0)
            * live[:, None, None]
        )
        share = share.astype(jnp.bfloat16)
        used = jnp.einsum("hu,kut->hkt", act_b, share, preferred_element_type=jnp.float32)
        onehot = (ids_b[:, None] == columns[None, :]).astype(jnp.float32)
        return (total + jnp.einsum("hkt,kn->hnt", used, onehot), None)

    total, _ = lax.scan(one_block, init, (acts.transpose(1, 0, 2), tiles, id_rows, count_rows))
    return total.reshape(hours, camp_blocks * tile)


def on_device(scores, elig_ids, elig_counts, activity, prices, spend_limit):
    entries = prices.size * lax.axis_size(USERS) * lax.axis_size("camps")

    def direction_at(lam):
        group_bf = gathered_copies(lam.astype(jnp.bfloat16), USERS, 1)
        partial_value = local_usage(group_bf, scores, elig_ids, elig_counts, activity)
        usage = sum_at_owner(partial_value, USERS, 1)
        gap = usage - spend_limit
        squares = over_axes(jnp.sum(gap * gap), USERS_CAMPS)
        return gap * lax.rsqrt(squares / entries + 1e-06)

    lam = prices
    last = prices
    for step in range(STEPS):
        middle = jnp.maximum(lam + 0.3 * direction_at(lam), 0.0)
        last = direction_at(middle)
        extra = jnp.maximum(lam + 0.3 * last, 0.0)
        weight = 1.0 / (step + 2.0)
        lam = weight * prices + (1.0 - weight) * extra
    return (lam, last)


def solution(mesh):
    torus = Mesh(
        mesh.devices.reshape(4, 4, 2, mesh.shape["camps"]),
        ("users_0", "users_1", "users_2", "camps"),
    )
    in_specs = (
        P(USERS, "camps", None, None, None),
        P(USERS, "camps", None),
        P(USERS, "camps"),
        P(None, USERS),
        P(None, USERS_CAMPS),
        P(None, USERS_CAMPS),
    )
    out_specs = (P(None, USERS_CAMPS), P(None, USERS_CAMPS))
    return jax.shard_map(
        on_device, mesh=torus, in_specs=in_specs, out_specs=out_specs, check_vma=False
    )
```

profile of v0, /device:TPU:1, one launch (start us, length us, event | category | flops | bytes accessed | tf_op | source)
XLA Modules:
  0.0 375.5 jit_solution(7792770455053726349)
XLA Ops:
  0.6 0.8 convert_element_type.80
  1.5 0.8 broadcast_in_dim.23
  2.2 10.4 %all-to-all-start = ((bf16[32,24,256]{2,1,0:T(8,128)(2,1)}), bf16[32,24,256]{2,1,0:T(8,128)(2,1)S(1)}, u32[]{:S(2)}, u32[]{:S(2)}) async-start(bf16[32,24,256]{2,1,0:T(8,128)(2,1)} %broadcast_in_dim.23), calls=%async_computation | async-start | bytes 786432 | tf_op jit(solution)/shard_map/all_to_all | solution.py:16
  13.3 9.5 %all-to-all-done = bf16[32,24,256]{2,1,0:T(8,128)(2,1)S(1)} async-done(((bf16[32,24,256]{2,1,0:T(8,128)(2,1)}), bf16[32,24,256]{2,1,0:T(8,128)(2,1)S(1)}, u32[]{:S(2)}, u32[]{:S(2)}) %all-to-all-start) | async-done | bytes 393248 | tf_op jit(solution)/shard_map/all_to_all | solution.py:16
  23.4 0.7 copy-done.3
  24.0 6.0 %while.44 = (s32[]{:T(128)}, f32[24,64,128]{2,1,0:T(8,128)S(1)}, s32[2,12]{1,0:T(2,128)S(1)}, bf16[2,24,128]{2,1,0:T(8,128)(2,1)S(1)}, bf16[2,12,128,128]{2,3,1,...) while((s32[]{:T(128)}, f32[24,64,128]{2,1,0:T(8,128)S(1)}, ...), condition=%wide.region_1.3_spmd.clone, body=%wide.region_0.2_spmd.clone.sunk | while | flops 25401224 | bytes 2354183 | solution.py:74
  24.6 0.7 compare_and_fusion.8
  25.9 0.7 fusion.210
  27.1 0.6 dynamic_slice.147
  27.6 0.7 compare_and_fusion.8
  28.9 0.7 fusion.210
  30.8 17.8 %all_to_all.40 = f32[32,24,256]{2,1,0:T(8,128)S(1)} all-to-all(f32[32,24,256]{2,1,0:T(8,128)S(1)} %copy.62), channel_id=1, replica_groups=mesh['users_0'=4,'users_1'=4,'users_2'=2,'camps'=16] {'users_0','users_1..., dimensions={0} | all-to-all | bytes 1572864 | tf_op jit(solution)/shard_map/all_to_all | solution.py:37
  48.6 0.7 copy-done.2
  49.3 0.6 multiply_reduce_fusion.3
  49.9 7.1 %psum.112 = f32[]{:T(128)} all-reduce(f32[]{:T(128)} %get-tuple-element.491), channel_id=1, replica_groups=mesh['users_0'=4,'users_1'=4,'users_2'=2,'camps'=16] {'users_0'}, use_global_device_ids=true, to_apply=%region_4.6 | all-reduce | flops 1 | bytes 8 | tf_op jit(solution)/shard_map/psum | solution.py:42
  57.0 8.8 %psum.113 = f32[]{:T(128)} all-reduce(f32[]{:T(128)} %psum.112), channel_id=1, replica_groups=mesh['users_0'=4,'users_1'=4,'users_2'=2,'camps'=16] {'users_1'}, use_global_device_ids=true, to_apply=%region_5.7 | all-reduce | flops 1 | bytes 8 | tf_op jit(solution)/shard_map/psum | solution.py:42
  65.8 5.9 %psum.114 = f32[]{:T(128)} all-reduce(f32[]{:T(128)} %psum.113), channel_id=1, replica_groups=mesh['users_0'=4,'users_1'=4,'users_2'=2,'camps'=16] {'users_2'}, use_global_device_ids=true, to_apply=%region_6.8 | all-reduce | flops 1 | bytes 8 | tf_op jit(solution)/shard_map/psum | solution.py:42
  71.7 28.0 %psum.115 = f32[]{:T(128)} all-reduce(f32[]{:T(128)} %psum.114), channel_id=1, replica_groups=mesh['users_0'=4,'users_1'=4,'users_2'=2,'camps'=16] {'camps'}, use_global_device_ids=true, to_apply=%region_7.9 | all-reduce | flops 1 | bytes 8 | tf_op jit(solution)/shard_map/psum | solution.py:42
  100.4 0.8 broadcast_in_dim.27
  101.1 11.1 %all-to-all-start.2 = ((bf16[32,24,256]{2,1,0:T(8,128)(2,1)}), bf16[32,24,256]{2,1,0:T(8,128)(2,1)S(1)}, u32[]{:S(2)}, u32[]{:S(2)}) async-start(bf16[32,24,256]{2,1,0:T(8,128)(2,1)} %broadcast_in_dim.27), calls=%async_computation.2 | async-start | bytes 786432 | tf_op jit(solution)/shard_map/all_to_all | solution.py:16
  112.3 10.2 %all-to-all-done.2 = bf16[32,24,256]{2,1,0:T(8,128)(2,1)S(1)} async-done(((bf16[32,24,256]{2,1,0:T(8,128)(2,1)}), bf16[32,24,256]{2,1,0:T(8,128)(2,1)S(1)}, u32[]{:S(2)}, u32[]{:S(2)}) %all-to-all-start.2) | async-done | bytes 393248 | tf_op jit(solution)/shard_map/all_to_all | solution.py:16
  123.0 6.1 %while.45 = (s32[]{:T(128)}, f32[24,64,128]{2,1,0:T(8,128)S(1)}, s32[2,12]{1,0:T(2,128)S(1)}, bf16[2,24,128]{2,1,0:T(8,128)(2,1)S(1)}, bf16[2,12,128,128]{2,3,1,...) while((s32[]{:T(128)}, f32[24,64,128]{2,1,0:T(8,128)S(1)}, ...), condition=%wide.region_9.11_spmd.clone, body=%wide.region_8.10_spmd.clone.sunk | while | flops 25401224 | bytes 2354183 | solution.py:74
  123.0 0.6 dynamic_slice.151
  123.6 0.7 compare_and_fusion.9
  124.9 0.7 fusion.217
  126.0 0.6 dynamic_slice.151
  126.6 0.7 compare_and_fusion.9
  127.9 0.7 fusion.217
  129.8 17.7 %all_to_all.41 = f32[32,24,256]{2,1,0:T(8,128)S(1)} all-to-all(f32[32,24,256]{2,1,0:T(8,128)S(1)} %copy.66), channel_id=1, replica_groups=mesh['users_0'=4,'users_1'=4,'users_2'=2,'camps'=16] {'users_0','users_1..., dimensions={0} | all-to-all | bytes 1572864 | tf_op jit(solution)/shard_map/all_to_all | solution.py:37
  147.6 0.6 multiply_reduce_fusion.2
  148.2 7.1 %psum.116 = f32[]{:T(128)} all-reduce(f32[]{:T(128)} %get-tuple-element.489), channel_id=1, replica_groups=mesh['users_0'=4,'users_1'=4,'users_2'=2,'camps'=16] {'users_0'}, use_global_device_ids=true, to_apply=%region_12.14 | all-reduce | flops 1 | bytes 8 | tf_op jit(solution)/shard_map/psum | solution.py:42
  155.3 8.8 %psum.117 = f32[]{:T(128)} all-reduce(f32[]{:T(128)} %psum.116), channel_id=1, replica_groups=mesh['users_0'=4,'users_1'=4,'users_2'=2,'camps'=16] {'users_1'}, use_global_device_ids=true, to_apply=%region_13.15 | all-reduce | flops 1 | bytes 8 | tf_op jit(solution)/shard_map/psum | solution.py:42
  164.1 5.9 %psum.118 = f32[]{:T(128)} all-reduce(f32[]{:T(128)} %psum.117), channel_id=1, replica_groups=mesh['users_0'=4,'users_1'=4,'users_2'=2,'camps'=16] {'users_2'}, use_global_device_ids=true, to_apply=%region_14.16 | all-reduce | flops 1 | bytes 8 | tf_op jit(solution)/shard_map/psum | solution.py:42
  170.0 20.8 %psum.119 = f32[]{:T(128)} all-reduce(f32[]{:T(128)} %psum.118), channel_id=1, replica_groups=mesh['users_0'=4,'users_1'=4,'users_2'=2,'camps'=16] {'camps'}, use_global_device_ids=true, to_apply=%region_15.17 | all-reduce | flops 1 | bytes 8 | tf_op jit(solution)/shard_map/psum | solution.py:42
  191.4 0.8 broadcast_in_dim.28
  192.2 10.7 %all-to-all-start.4 = ((bf16[32,24,256]{2,1,0:T(8,128)(2,1)}), bf16[32,24,256]{2,1,0:T(8,128)(2,1)S(1)}, u32[]{:S(2)}, u32[]{:S(2)}) async-start(bf16[32,24,256]{2,1,0:T(8,128)(2,1)} %broadcast_in_dim.28), calls=%async_computation.4 | async-start | bytes 786432 | tf_op jit(solution)/shard_map/all_to_all | solution.py:16
  203.0 10.2 %all-to-all-done.4 = bf16[32,24,256]{2,1,0:T(8,128)(2,1)S(1)} async-done(((bf16[32,24,256]{2,1,0:T(8,128)(2,1)}), bf16[32,24,256]{2,1,0:T(8,128)(2,1)S(1)}, u32[]{:S(2)}, u32[]{:S(2)}) %all-to-all-start.4) | async-done | bytes 393248 | tf_op jit(solution)/shard_map/all_to_all | solution.py:16
  213.7 6.1 %while.46 = (s32[]{:T(128)}, f32[24,64,128]{2,1,0:T(8,128)S(1)}, s32[2,12]{1,0:T(2,128)S(1)}, bf16[2,24,128]{2,1,0:T(8,128)(2,1)S(1)}, bf16[2,12,128,128]{2,3,1,...) while((s32[]{:T(128)}, f32[24,64,128]{2,1,0:T(8,128)S(1)}, ...), condition=%wide.region_17.19_spmd.clone, body=%wide.region_16.18_spmd.clone.sunk | while | flops 25401224 | bytes 2354183 | solution.py:74
  213.7 0.6 dynamic_slice.155
  214.3 0.7 compare_and_fusion.10
  215.6 0.7 fusion.224
  217.3 0.7 compare_and_fusion.10
  218.6 0.7 fusion.224
  220.5 17.8 %all_to_all.42 = f32[32,24,256]{2,1,0:T(8,128)S(1)} all-to-all(f32[32,24,256]{2,1,0:T(8,128)S(1)} %copy.70), channel_id=1, replica_groups=mesh['users_0'=4,'users_1'=4,'users_2'=2,'camps'=16] {'users_0','users_1..., dimensions={0} | all-to-all | bytes 1572864 | tf_op jit(solution)/shard_map/all_to_all | solution.py:37
  238.3 0.6 multiply_reduce_fusion.1
  238.9 7.1 %psum.120 = f32[]{:T(128)} all-reduce(f32[]{:T(128)} %get-tuple-element.487), channel_id=1, replica_groups=mesh['users_0'=4,'users_1'=4,'users_2'=2,'camps'=16] {'users_0'}, use_global_device_ids=true, to_apply=%region_20.22 | all-reduce | flops 1 | bytes 8 | tf_op jit(solution)/shard_map/psum | solution.py:42
  246.0 8.8 %psum.121 = f32[]{:T(128)} all-reduce(f32[]{:T(128)} %psum.120), channel_id=1, replica_groups=mesh['users_0'=4,'users_1'=4,'users_2'=2,'camps'=16] {'users_1'}, use_global_device_ids=true, to_apply=%region_21.23 | all-reduce | flops 1 | bytes 8 | tf_op jit(solution)/shard_map/psum | solution.py:42
  254.8 5.9 %psum.122 = f32[]{:T(128)} all-reduce(f32[]{:T(128)} %psum.121), channel_id=1, replica_groups=mesh['users_0'=4,'users_1'=4,'users_2'=2,'camps'=16] {'users_2'}, use_global_device_ids=true, to_apply=%region_22.24 | all-reduce | flops 1 | bytes 8 | tf_op jit(solution)/shard_map/psum | solution.py:42
  260.7 22.5 %psum.123 = f32[]{:T(128)} all-reduce(f32[]{:T(128)} %psum.122), channel_id=1, replica_groups=mesh['users_0'=4,'users_1'=4,'users_2'=2,'camps'=16] {'camps'}, use_global_device_ids=true, to_apply=%region_23.25 | all-reduce | flops 1 | bytes 8 | tf_op jit(solution)/shard_map/psum | solution.py:42
  283.9 0.8 broadcast_in_dim.29
  284.7 11.0 %all-to-all-start.6 = ((bf16[32,24,256]{2,1,0:T(8,128)(2,1)}), bf16[32,24,256]{2,1,0:T(8,128)(2,1)S(1)}, u32[]{:S(2)}, u32[]{:S(2)}) async-start(bf16[32,24,256]{2,1,0:T(8,128)(2,1)} %broadcast_in_dim.29), calls=%async_computation.6 | async-start | bytes 786432 | tf_op jit(solution)/shard_map/all_to_all | solution.py:16
  295.7 10.2 %all-to-all-done.6 = bf16[32,24,256]{2,1,0:T(8,128)(2,1)S(1)} async-done(((bf16[32,24,256]{2,1,0:T(8,128)(2,1)}), bf16[32,24,256]{2,1,0:T(8,128)(2,1)S(1)}, u32[]{:S(2)}, u32[]{:S(2)}) %all-to-all-start.6) | async-done | bytes 393248 | tf_op jit(solution)/shard_map/all_to_all | solution.py:16
  306.4 6.1 %while.47 = (s32[]{:T(128)}, f32[24,64,128]{2,1,0:T(8,128)S(1)}, s32[2,12]{1,0:T(2,128)S(1)}, bf16[2,24,128]{2,1,0:T(8,128)(2,1)S(1)}, bf16[2,12,128,128]{2,3,1,...) while((s32[]{:T(128)}, f32[24,64,128]{2,1,0:T(8,128)S(1)}, ...), condition=%wide.region_25.27_spmd.clone, body=%wide.region_24.26_spmd.clone.sunk | while | flops 25401224 | bytes 2354183 | solution.py:74
  307.0 0.7 compare_and_fusion.11
  308.3 0.7 fusion.231
  310.1 0.7 compare_and_fusion.11
  311.3 0.7 fusion.231
  313.2 17.8 %all_to_all.43 = f32[32,24,256]{2,1,0:T(8,128)S(1)} all-to-all(f32[32,24,256]{2,1,0:T(8,128)S(1)} %copy.74), channel_id=1, replica_groups=mesh['users_0'=4,'users_1'=4,'users_2'=2,'camps'=16] {'users_0','users_1..., dimensions={0} | all-to-all | bytes 1572864 | tf_op jit(solution)/shard_map/all_to_all | solution.py:37
  331.0 0.6 multiply_reduce_fusion
  331.6 7.1 %psum.124 = f32[]{:T(128)} all-reduce(f32[]{:T(128)} %get-tuple-element.485), channel_id=1, replica_groups=mesh['users_0'=4,'users_1'=4,'users_2'=2,'camps'=16] {'users_0'}, use_global_device_ids=true, to_apply=%region_28.30 | all-reduce | flops 1 | bytes 8 | tf_op jit(solution)/shard_map/psum | solution.py:42
  338.7 8.8 %psum.125 = f32[]{:T(128)} all-reduce(f32[]{:T(128)} %psum.124), channel_id=1, replica_groups=mesh['users_0'=4,'users_1'=4,'users_2'=2,'camps'=16] {'users_1'}, use_global_device_ids=true, to_apply=%region_29.31 | all-reduce | flops 1 | bytes 8 | tf_op jit(solution)/shard_map/psum | solution.py:42
  347.5 5.9 %psum.126 = f32[]{:T(128)} all-reduce(f32[]{:T(128)} %psum.125), channel_id=1, replica_groups=mesh['users_0'=4,'users_1'=4,'users_2'=2,'camps'=16] {'users_2'}, use_global_device_ids=true, to_apply=%region_30.32 | all-reduce | flops 1 | bytes 8 | tf_op jit(solution)/shard_map/psum | solution.py:42
  353.4 20.8 %psum.127 = f32[]{:T(128)} all-reduce(f32[]{:T(128)} %psum.126), channel_id=1, replica_groups=mesh['users_0'=4,'users_1'=4,'users_2'=2,'camps'=16] {'camps'}, use_global_device_ids=true, to_apply=%region_31.33 | all-reduce | flops 1 | bytes 8 | tf_op jit(solution)/shard_map/psum | solution.py:42
  374.9 0.6 multiply_add_fusion
  (80 shorter events, 16.4 us)
Async XLA Ops:
  0.6 12.0 %copy-start = (bf16[2,1,12,128,128]{4,3,2,1,0:T(8,128)(2,1)S(1)}, bf16[2,1,12,128,128]{4,3,2,1,0:T(8,128)(2,1)}, u32[]{:S(2)}) copy-start(bf16[2,1,12,128,128]{4,3,2,1,0:T(8,128)(2,1)} %param.16) | copy-start | bytes 2359300
  2.2 20.6 %all-to-all-start = ((bf16[32,24,256]{2,1,0:T(8,128)(2,1)}), bf16[32,24,256]{2,1,0:T(8,128)(2,1)S(1)}, u32[]{:S(2)}, u32[]{:S(2)}) async-start(bf16[32,24,256]{2,1,0:T(8,128)(2,1)} %broadcast_in_dim.23), calls=%async_computation | async-start | bytes 786432 | tf_op jit(solution)/shard_map/all_to_all | solution.py:16
  12.6 0.7 copy-start.4
  23.3 0.7 copy-start.3
  23.4 0.7 copy-start.5
  48.5 0.7 copy-start.2
  49.3 51.1 %copy-start.1 = (f32[24,256]{1,0:T(8,128)S(1)}, f32[24,256]{1,0:T(8,128)}, u32[]{:S(2)}) copy-start(f32[24,256]{1,0:T(8,128)} %param.20) | copy-start | bytes 73732
  101.1 21.4 %all-to-all-start.2 = ((bf16[32,24,256]{2,1,0:T(8,128)(2,1)}), bf16[32,24,256]{2,1,0:T(8,128)(2,1)S(1)}, u32[]{:S(2)}, u32[]{:S(2)}) async-start(bf16[32,24,256]{2,1,0:T(8,128)(2,1)} %broadcast_in_dim.27), calls=%async_computation.2 | async-start | bytes 786432 | tf_op jit(solution)/shard_map/all_to_all | solution.py:16
  192.2 21.0 %all-to-all-start.4 = ((bf16[32,24,256]{2,1,0:T(8,128)(2,1)}), bf16[32,24,256]{2,1,0:T(8,128)(2,1)S(1)}, u32[]{:S(2)}, u32[]{:S(2)}) async-start(bf16[32,24,256]{2,1,0:T(8,128)(2,1)} %broadcast_in_dim.28), calls=%async_computation.4 | async-start | bytes 786432 | tf_op jit(solution)/shard_map/all_to_all | solution.py:16
  284.7 21.3 %all-to-all-start.6 = ((bf16[32,24,256]{2,1,0:T(8,128)(2,1)}), bf16[32,24,256]{2,1,0:T(8,128)(2,1)S(1)}, u32[]{:S(2)}, u32[]{:S(2)}) async-start(bf16[32,24,256]{2,1,0:T(8,128)(2,1)} %broadcast_in_dim.29), calls=%async_computation.6 | async-start | bytes 786432 | tf_op jit(solution)/shard_map/all_to_all | solution.py:16
where the time goes:
time: 383 us; the launch traced here: 375 us
  blocking collectives  250 us (65%)
  starting transfers between devices  43.2 us (11%)
  waiting for transfers between devices  40.2 us (10%)
  local copies, waits for them, and re-layouts  19 us (5%)
  other arithmetic  9.48 us (2%)
  matrix products  9.17 us (2%)
    psum x16, blocking collectives, over_axes(): return functools.reduce(lax.psum, axes, value)  179 us
    all_to_all x4, blocking collectives, sum_at_owner(): lax.all_to_all(parts, axis, split_axis=0, concat_axis=0, tiled=True)  71 us
    all_to_all x4, starting transfers between devices, sent_to_all(): return lax.all_to_all(copies, axis, split_axis=0, concat_axis=0, tiled=True)  43.2 us
    all_to_all x4, waiting for transfers between devices, sent_to_all(): return lax.all_to_all(copies, axis, split_axis=0, concat_axis=0, tiled=True)  40.2 us
  transfers between devices with their start and end apart: 4, of which 4 were waited for; matrix products, arithmetic and copies ran while one was open for 0% of the time, Pallas kernels for 0%

commit v1 on v0

v1 whole, which is shorter than its diff:
```python
import functools

import jax
import jax.numpy as jnp
from jax import lax
from jax.experimental import pallas as pl
from jax.experimental.pallas import tpu as pltpu
from jax.sharding import Mesh
from jax.sharding import PartitionSpec as P

STEPS = 2
USERS = ("users_0", "users_1", "users_2")
USERS_CAMPS = ("users_0", "users_1", "users_2", "camps")
TILE = 128
ACT = 32
FLAGS = 8
UNROLL = 4

VMEM = pl.BlockSpec(memory_space=pltpu.VMEM)
SMEM = pl.BlockSpec(memory_space=pltpu.SMEM)


def packet_rows(blocks, owned):
    return blocks * owned * TILE + blocks * ACT + FLAGS


def pack_kernel(owned, ids_ref, counts_ref, scores_ref, act_ref, out_ref):
    devices = out_ref.shape[0]
    hours = act_ref.shape[0]
    blocks, slots = scores_ref.shape[0], scores_ref.shape[1]
    acts = blocks * owned * TILE
    flags = acts + blocks * ACT
    hour = lax.broadcasted_iota(jnp.int32, (ACT - hours, TILE), 0)
    ones = jnp.where(hour == 0, 1.0, 0.0).astype(jnp.bfloat16)
    lane = lax.broadcasted_iota(jnp.int32, (FLAGS, TILE), 1)
    tails = [
        jnp.concatenate([act_ref[:, b * TILE : (b + 1) * TILE], ones], axis=0)
        for b in range(blocks)
    ]
    for dev in range(devices):
        for b in range(blocks):
            out_ref[dev, acts + b * ACT : acts + (b + 1) * ACT, :] = tails[b]
        out_ref[dev, flags : flags + FLAGS, :] = jnp.zeros((FLAGS, TILE), jnp.bfloat16)

    for b in range(blocks):

        @pl.loop(0, jnp.minimum(counts_ref[b], slots))
        def _(k):
            where = ids_ref[b, k]
            dev = where // owned
            slot = b * owned + lax.rem(where, owned)
            row = pl.multiple_of(slot * TILE, TILE)
            out_ref[dev, pl.ds(row, TILE), :] = scores_ref[b, k]
            mark = jnp.where(lane == slot, 1.0, 0.0).astype(jnp.bfloat16)
            out_ref[dev, flags : flags + FLAGS, :] += mark


def list_kernel(blocks, owned, flags_ref, list_ref):
    devices = flags_ref.shape[0]
    span = list_ref.shape[1]
    for t in range(owned):

        def add(i, n, t=t):
            for b in range(blocks):
                list_ref[t, n + 1] = i * blocks + b
                n = n + flags_ref[i, b * owned + t]
            return n

        n = lax.fori_loop(0, devices, add, jnp.int32(0))
        last = list_ref[t, jnp.maximum(n, 1)]
        for p in range(UNROLL):
            list_ref[t, jnp.minimum(n + 1 + p, span - 1)] = last
        list_ref[t, 0] = n


def local_usage(owned, lam, list_ref, packets_ref):
    hours = lam.shape[0]
    rows = packets_ref.shape[1]
    blocks = (rows - FLAGS) // (owned * TILE + ACT)
    acts = blocks * owned * TILE
    hour = lax.broadcasted_iota(jnp.int32, (ACT - hours, TILE), 0)
    half = jnp.where(hour == 0, 0.5, 0.0).astype(jnp.bfloat16)
    usages = []
    for t in range(owned):
        rounded = lam[:, t * TILE : (t + 1) * TILE].astype(jnp.bfloat16)
        weights = jnp.concatenate([rounded * jnp.bfloat16(-0.5), half], axis=0)
        count = list_ref[t, 0]

        def group(g, total, t=t, weights=weights, count=count):
            for p in range(UNROLL):
                at = g * UNROLL + p
                entry = list_ref[t, at + 1]
                dev = entry // blocks
                b = lax.rem(entry, blocks)
                act_row = pl.multiple_of(acts + b * ACT, ACT)
                act = packets_ref[dev, pl.ds(act_row, ACT), :]
                row = pl.multiple_of((b * owned + t) * TILE, TILE)
                score = packets_ref[dev, pl.ds(row, TILE), :].astype(jnp.float32)
                part = lax.dot_general(
                    act, weights, (((0,), (0,)), ((), ())), preferred_element_type=jnp.float32
                )
                share = jnp.clip(score * 0.5 + part, 0.0, 1.0).astype(jnp.bfloat16)
                live = jnp.where(at < count, 1.0, 0.0).astype(jnp.bfloat16)
                total = total + jnp.dot(act * live, share, preferred_element_type=jnp.float32)
            return total

        groups = (count + UNROLL - 1) // UNROLL
        total = lax.fori_loop(0, groups, group, jnp.zeros((ACT, TILE), jnp.float32))
        usages.append(total[:hours])
    return jnp.concatenate(usages, axis=1)


def scale_of(parts_ref, entries):
    squares = jnp.sum(jnp.sum(parts_ref[:, 0, :], axis=0, keepdims=True), axis=1, keepdims=True)
    return lax.rsqrt(squares / entries + 1e-06)


def moved(lam, gap, scale):
    return jnp.maximum(lam + 0.3 * (gap * scale), 0.0)


def direction_kernel(owned, entries, kind, *refs):
    if kind == "first":
        list_ref, packets_ref, limit_ref, lam_ref, gap_ref, parts_ref = refs
        at = lam_ref[...]
    elif kind == "middle":
        list_ref, packets_ref, limit_ref, lam_ref, before_ref, sums_ref, gap_ref, parts_ref = refs
        at = moved(lam_ref[...], before_ref[...], scale_of(sums_ref, entries))
    else:
        (list_ref, packets_ref, limit_ref, anchor_ref, lam_ref, before_ref, sums_ref) = refs[:7]
        gap_ref, parts_ref, lam_out_ref = refs[7:]
        extra = moved(lam_ref[...], before_ref[...], scale_of(sums_ref, entries))
        weight = 1.0 / (kind + 2.0)
        at = weight * anchor_ref[...] + (1.0 - weight) * extra
        lam_out_ref[...] = at
    gap = local_usage(owned, at, list_ref, packets_ref) - limit_ref[...]
    gap_ref[...] = gap
    squares = gap * gap
    line = sum(squares[:, t * TILE : (t + 1) * TILE] for t in range(owned))
    line = jnp.sum(line, axis=0, keepdims=True)
    parts_ref[...] = jnp.broadcast_to(line[None], parts_ref.shape)


def final_kernel(entries, step, anchor_ref, lam_ref, gap_ref, sums_ref, new_ref, dir_ref):
    scale = scale_of(sums_ref, entries)
    gap = gap_ref[...]
    dir_ref[...] = gap * scale
    extra = moved(lam_ref[...], gap, scale)
    weight = 1.0 / (step + 2.0)
    new_ref[...] = weight * anchor_ref[...] + (1.0 - weight) * extra


def swapped(parts, axis):
    return lax.all_to_all(parts, axis, split_axis=0, concat_axis=0, tiled=True)


def on_device(scores, elig_ids, elig_counts, activity, prices, spend_limit):
    devices = lax.axis_size(USERS)
    groups = lax.axis_size("camps")
    entries = float(prices.size * devices * groups)
    hours, piece = prices.shape
    owned = piece // TILE
    blocks = scores.shape[0]
    rows = packet_rows(blocks, owned)
    params = pltpu.CompilerParams(vmem_limit_bytes=8 * 2**20)

    packets = pl.pallas_call(
        functools.partial(pack_kernel, owned),
        out_shape=jax.ShapeDtypeStruct((devices, rows, TILE), jnp.bfloat16),
        in_specs=[SMEM, SMEM, VMEM, VMEM],
        out_specs=VMEM,
        compiler_params=params,
        name="pack",
    )(elig_ids[:, 0], elig_counts[:, 0], scores[:, 0], activity)
    packets = swapped(packets, USERS)
    flags = packets[:, rows - FLAGS, : blocks * owned].astype(jnp.int32)
    lists = pl.pallas_call(
        functools.partial(list_kernel, blocks, owned),
        out_shape=jax.ShapeDtypeStruct((owned, devices * blocks + 1 + UNROLL), jnp.int32),
        in_specs=[SMEM],
        out_specs=SMEM,
        compiler_params=params,
        name="lists",
    )(flags)

    value = jax.ShapeDtypeStruct(prices.shape, jnp.float32)
    parts = jax.ShapeDtypeStruct((devices, 1, TILE), jnp.float32)

    def direction(kind, *args):
        outs = [value, parts] + ([value] if kind not in ("first", "middle") else [])
        got = pl.pallas_call(
            functools.partial(direction_kernel, owned, entries, kind),
            out_shape=outs,
            in_specs=[SMEM] + [VMEM] * (len(args) + 2),
            out_specs=[VMEM] * len(outs),
            compiler_params=params,
            name="direction",
        )(lists, packets, spend_limit, *args)
        over_users = swapped(got[1], USERS).sum(axis=0)
        sums = swapped(jnp.broadcast_to(over_users[None], (groups, 1, TILE)), "camps")
        return got[0], sums, got[2:]

    lam = prices
    gap, sums, _ = direction("first", lam)
    for step in range(STEPS):
        gap, sums, _ = direction("middle", lam, gap, sums)
        if step < STEPS - 1:
            gap, sums, (lam,) = direction(step, prices, lam, gap, sums)
    new, last = pl.pallas_call(
        functools.partial(final_kernel, entries, STEPS - 1),
        out_shape=[value, value],
        in_specs=[VMEM] * 4,
        out_specs=[VMEM] * 2,
        compiler_params=params,
        name="final",
    )(prices, lam, gap, sums)
    return (new, last)


def solution(mesh):
    torus = Mesh(
        mesh.devices.reshape(4, 4, 2, mesh.shape["camps"]),
        ("users_0", "users_1", "users_2", "camps"),
    )
    in_specs = (
        P(USERS, "camps", None, None, None),
        P(USERS, "camps", None),
        P(USERS, "camps"),
        P(None, USERS),
        P(None, USERS_CAMPS),
        P(None, USERS_CAMPS),
    )
    out_specs = (P(None, USERS_CAMPS), P(None, USERS_CAMPS))
    return jax.shard_map(
        on_device, mesh=torus, in_specs=in_specs, out_specs=out_specs, check_vma=False
    )
```

time: 383 us -> 207 us (0.54); the launches traced: 375 us -> 207 us
  blocking collectives: 250 us -> 180 us
  starting transfers between devices: 43.2 us -> 0 us
  waiting for transfers between devices: 40.2 us -> 0 us
  Pallas kernels: 0 us -> 13.6 us
  other arithmetic: 9.48 us -> 0.22 us
  matrix products: 9.17 us -> 0 us
  local copies, waits for them, and re-layouts: 19 us -> 12.4 us
    psum x16 -> x0, blocking collectives: 179 us -> none  [over_axes(): return functools.reduce(lax.psum, axes, value)]
    all_to_all x4 -> x9, blocking collectives: 71 us -> 180 us  [swapped(): return lax.all_to_all(parts, axis, split_axis=0, concat_axis=0, tiled=True)]
    all_to_all x4 -> x0, starting transfers between devices: 43.2 us -> none  [sent_to_all(): return lax.all_to_all(copies, axis, split_axis=0, concat_axis=0, tiled=True)]
    all_to_all x4 -> x0, waiting for transfers between devices: 40.2 us -> none  [sent_to_all(): return lax.all_to_all(copies, axis, split_axis=0, concat_axis=0, tiled=True)]
    pallas_call x0 -> x7, Pallas kernels: none -> 13.6 us  [the longest x4 9.96 us: direction(): pl.pallas_call(functools.partial(direction_kernel, owned, entries, kind),...]
    unnamed x18 -> x20, local copies, waits for them, and re-layouts: 3.09 us -> 12.4 us
    dot_general x16 -> x0, matrix products: 9.17 us -> none  [the longest x8 5.38 us: one_block(): jnp.einsum('hu,kut->hkt', act_b, share, preferred_element_type=jnp.float32)]
    and x8 -> x0, other arithmetic: 5.25 us -> none  [one_block(): picked = jnp.take(table, ids_b, axis=1)]
  transfers between devices with their start and end apart: 4 -> 0, of which waited for: 4 -> 0; matrix products, arithmetic and copies ran while one was open for 0% -> 0% of each run, Pallas kernels for 0% -> 0%
where the time goes in v1:
time: 207 us
  blocking collectives  180 us (87%)
  Pallas kernels  13.6 us (7%)
  local copies, waits for them, and re-layouts  12.4 us (6%)
    all_to_all x9, blocking collectives, swapped(): return lax.all_to_all(parts, axis, split_axis=0, concat_axis=0, tiled=True)  180 us
    unnamed x20, local copies, waits for them, and re-layouts  12.4 us
    pallas_call x4, Pallas kernels, direction(): pl.pallas_call(functools.partial(direction_kernel, owned, entries, kind),...  9.96 us

profile of v1, /device:TPU:1, one launch (start us, length us, event | category | flops | bytes accessed | tf_op | source)
XLA Modules:
  0.0 206.7 jit_solution(10541392759772872060)
XLA Ops:
  0.6 0.0 copy-start.4
  0.6 1.1 copy-done.4
  1.8 0.0 copy-start.7
  1.8 0.7 copy-done.7
  2.5 0.0 copy-start.8
  2.5 0.7 copy-done.8
  3.2 0.0 copy-start.9
  3.2 0.7 copy-done.9
  3.8 0.9 pack.1
  4.7 0.0 copy-start.5
  4.8 0.0 copy-start.6
  4.8 66.8 %all_to_all.45.refs_1_ = bf16[32,584,128]{2,1,0:T(8,128)(2,1)S(1)} all-to-all(bf16[32,584,128]{2,1,0:T(8,128)(2,1)S(1)} %pack.1), channel_id=1, replica_groups=mesh['users_0'=4,'users_1'=4,'users_2'=2,'camps'=16] {'users_0','users_1..., dimensions={0} | all-to-all | bytes 9568256 | tf_op jit(solution)/shard_map/all_to_all | solution.py:154
  71.6 2.0 lists.1.refs_0_
  73.6 0.0 copy-done.5
  73.6 0.0 copy-done.6
  73.6 2.4 %direction.4 = (f32[24,256]{1,0:T(8,128)S(1)}, f32[32,1,128]{2,1,0:T(1,128)S(1)}) custom-call(s32[2,69]{1,0:T(2,128)S(1)} %lists.1.refs_0_, bf16[32,584,128]{2,1,0:T(8,128)(2,1)S(1)} %all_to_all.45.refs_1_, f32[24,256]{1,0:T(8,128)S(1)} %copy-done.6, f32[24,256]{1,0:T(8,128)S(1)} %copy-done.5), custom_call_target="tpu_custom_call" | custom-call | tf_op jit(solution)/shard_map/direction/pallas_call | solution.py:191
  76.0 0.0 copy-start
  76.0 2.1 %copy-done = bf16[32,584,128]{2,1,0:T(8,128)(2,1)} copy-done((bf16[32,584,128]{2,1,0:T(8,128)(2,1)}, bf16[32,584,128]{2,1,0:T(8,128)(2,1)S(1)}, u32[]{:S(2)}) %copy-start) | copy-done | bytes 4784152
  78.2 10.9 %all_to_all.46 = f32[32,1,128]{2,1,0:T(1,128)S(1)} all-to-all(f32[32,1,128]{2,1,0:T(1,128)S(1)} %get-tuple-element.12), channel_id=1, replica_groups=mesh['users_0'=4,'users_1'=4,'users_2'=2,'camps'=16] {'users_0','users_1..., dimensions={0} | all-to-all | bytes 32768 | tf_op jit(solution)/shard_map/all_to_all | solution.py:154
  89.0 0.1 reduce_sum.36
  89.1 24.8 %all_to_all.47.refs_5_ = f32[16,1,128]{2,1,0:T(1,128)S(1)} all-to-all(f32[16,1,128]{2,1,0:T(1,128)S(1)} %broadcast_in_dim.8), channel_id=1, replica_groups=mesh['users_0'=4,'users_1'=4,'users_2'=2,'camps'=16] {'camps'}, dimensions={0} | all-to-all | bytes 16384 | tf_op jit(solution)/shard_map/all_to_all | solution.py:154
  113.9 0.0 copy-start.1
  113.9 2.4 %copy-done.1 = bf16[32,584,128]{2,1,0:T(8,128)(2,1)S(1)} copy-done((bf16[32,584,128]{2,1,0:T(8,128)(2,1)S(1)}, bf16[32,584,128]{2,1,0:T(8,128)(2,1)}, u32[]{:S(2)}) %copy-start.1) | copy-done | bytes 4784152
  116.3 2.5 %direction.5 = (f32[24,256]{1,0:T(8,128)S(1)}, f32[32,1,128]{2,1,0:T(1,128)S(1)}) custom-call(s32[2,69]{1,0:T(2,128)S(1)} %lists.1.refs_0_, bf16[32,584,128]{2,1,0:T(8,128)(2,1)S(1)} %copy-done.1, f32[24,256]{1,0:T(8,128)S(1)} %copy-done.6, f32[24,256]{1,0:T(8,128)S(1)} %copy-done.5, f32[24,256]{1,0:T(8,128)S(1)} %get-tuple-element.11.refs_4_, ...), custom_call_target="tpu_custom_call" | custom-call | tf_op jit(solution)/shard_map/direction/pallas_call | solution.py:191
  118.8 12.1 %all_to_all.48 = f32[32,1,128]{2,1,0:T(1,128)S(1)} all-to-all(f32[32,1,128]{2,1,0:T(1,128)S(1)} %get-tuple-element.14), channel_id=1, replica_groups=mesh['users_0'=4,'users_1'=4,'users_2'=2,'camps'=16] {'users_0','users_1..., dimensions={0} | all-to-all | bytes 32768 | tf_op jit(solution)/shard_map/all_to_all | solution.py:154
  130.9 0.1 reduce_sum.37
  130.9 13.8 %all_to_all.49.refs_6_ = f32[16,1,128]{2,1,0:T(1,128)S(1)} all-to-all(f32[16,1,128]{2,1,0:T(1,128)S(1)} %broadcast_in_dim.9), channel_id=1, replica_groups=mesh['users_0'=4,'users_1'=4,'users_2'=2,'camps'=16] {'camps'}, dimensions={0} | all-to-all | bytes 16384 | tf_op jit(solution)/shard_map/all_to_all | solution.py:154
  144.8 0.0 copy-start.2
  144.8 2.4 %copy-done.2 = bf16[32,584,128]{2,1,0:T(8,128)(2,1)S(1)} copy-done((bf16[32,584,128]{2,1,0:T(8,128)(2,1)S(1)}, bf16[32,584,128]{2,1,0:T(8,128)(2,1)}, u32[]{:S(2)}) %copy-start.2) | copy-done | bytes 4784152
  147.1 2.5 %direction.6 = (f32[24,256]{1,0:T(8,128)S(1)}, f32[32,1,128]{2,1,0:T(1,128)S(1)}, f32[24,256]{1,0:T(8,128)S(1)}) custom-call(s32[2,69]{1,0:T(2,128)S(1)} %lists.1.refs_0_, bf16[32,584,128]{2,1,0:T(8,128)(2,1)S(1)} %copy-done.2, f32[24,256]{1,0:T(8,128)S(1)} %copy-done.6, f32[24,256]{1,0:T(8,128)S(1)} %copy-done.5, f32[24,256]{1,0:T(8,128)S(1)} %copy-done.5, ...), custom_call_target="tpu_custom_call" | custom-call | tf_op jit(solution)/shard_map/direction/pallas_call | solution.py:191
  149.7 11.8 %all_to_all.50 = f32[32,1,128]{2,1,0:T(1,128)S(1)} all-to-all(f32[32,1,128]{2,1,0:T(1,128)S(1)} %get-tuple-element.17), channel_id=1, replica_groups=mesh['users_0'=4,'users_1'=4,'users_2'=2,'camps'=16] {'users_0','users_1..., dimensions={0} | all-to-all | bytes 32768 | tf_op jit(solution)/shard_map/all_to_all | solution.py:154
  161.5 0.1 reduce_sum.38
  161.6 13.8 %all_to_all.51.refs_5_ = f32[16,1,128]{2,1,0:T(1,128)S(1)} all-to-all(f32[16,1,128]{2,1,0:T(1,128)S(1)} %broadcast_in_dim.10), channel_id=1, replica_groups=mesh['users_0'=4,'users_1'=4,'users_2'=2,'camps'=16] {'camps'}, dimensions={0} | all-to-all | bytes 16384 | tf_op jit(solution)/shard_map/all_to_all | solution.py:154
  175.4 0.0 copy-start.3
  175.4 2.4 %copy-done.3 = bf16[32,584,128]{2,1,0:T(8,128)(2,1)S(1)} copy-done((bf16[32,584,128]{2,1,0:T(8,128)(2,1)S(1)}, bf16[32,584,128]{2,1,0:T(8,128)(2,1)}, u32[]{:S(2)}) %copy-start.3) | copy-done | bytes 4784152
  177.8 2.5 %direction.7 = (f32[24,256]{1,0:T(8,128)S(1)}, f32[32,1,128]{2,1,0:T(1,128)S(1)}) custom-call(s32[2,69]{1,0:T(2,128)S(1)} %lists.1.refs_0_, bf16[32,584,128]{2,1,0:T(8,128)(2,1)S(1)} %copy-done.3, f32[24,256]{1,0:T(8,128)S(1)} %copy-done.6, f32[24,256]{1,0:T(8,128)S(1)} %get-tuple-element.15.refs_3_.lam_ref, f32[24,256]{1,0:T(8,128)S(1)} %get-tuple-element.16.refs_4_, ...), custom_call_target="tpu_custom_call" | custom-call | tf_op jit(solution)/shard_map/direction/pallas_call | solution.py:191
  180.3 11.8 %all_to_all.52 = f32[32,1,128]{2,1,0:T(1,128)S(1)} all-to-all(f32[32,1,128]{2,1,0:T(1,128)S(1)} %get-tuple-element.19), channel_id=1, replica_groups=mesh['users_0'=4,'users_1'=4,'users_2'=2,'camps'=16] {'users_0','users_1..., dimensions={0} | all-to-all | bytes 32768 | tf_op jit(solution)/shard_map/all_to_all | solution.py:154
  192.1 0.1 reduce_sum.39
  192.2 13.8 %all_to_all.53.sums_ref = f32[16,1,128]{2,1,0:T(1,128)S(1)} all-to-all(f32[16,1,128]{2,1,0:T(1,128)S(1)} %broadcast_in_dim.11), channel_id=1, replica_groups=mesh['users_0'=4,'users_1'=4,'users_2'=2,'camps'=16] {'camps'}, dimensions={0} | all-to-all | bytes 16384 | tf_op jit(solution)/shard_map/all_to_all | solution.py:154
  206.0 0.7 final.1
  (5 shorter events, 0.1 us)
Async XLA Ops:
  0.6 1.1 copy-start.4
  1.8 0.7 copy-start.7
  2.5 0.7 copy-start.8
  3.2 0.7 copy-start.9
  4.7 68.8 %copy-start.5 = (f32[24,256]{1,0:T(8,128)S(1)}, f32[24,256]{1,0:T(8,128)}, u32[]{:S(2)}) copy-start(f32[24,256]{1,0:T(8,128)} %anchor_ref.1) | copy-start | bytes 73732
  4.8 68.8 %copy-start.6 = (f32[24,256]{1,0:T(8,128)S(1)}, f32[24,256]{1,0:T(8,128)}, u32[]{:S(2)}) copy-start(f32[24,256]{1,0:T(8,128)} %refs_2_.7) | copy-start | bytes 73732
  76.0 2.1 %copy-start = (bf16[32,584,128]{2,1,0:T(8,128)(2,1)}, bf16[32,584,128]{2,1,0:T(8,128)(2,1)S(1)}, u32[]{:S(2)}) copy-start(bf16[32,584,128]{2,1,0:T(8,128)(2,1)S(1)} %all_to_all.45.refs_1_) | copy-start | bytes 14352388
  113.9 2.4 %copy-start.1 = (bf16[32,584,128]{2,1,0:T(8,128)(2,1)S(1)}, bf16[32,584,128]{2,1,0:T(8,128)(2,1)}, u32[]{:S(2)}) copy-start(bf16[32,584,128]{2,1,0:T(8,128)(2,1)} %copy-done) | copy-start | bytes 14352388
  144.8 2.4 %copy-start.2 = (bf16[32,584,128]{2,1,0:T(8,128)(2,1)S(1)}, bf16[32,584,128]{2,1,0:T(8,128)(2,1)}, u32[]{:S(2)}) copy-start(bf16[32,584,128]{2,1,0:T(8,128)(2,1)} %copy-done) | copy-start | bytes 14352388
  175.4 2.4 %copy-start.3 = (bf16[32,584,128]{2,1,0:T(8,128)(2,1)S(1)}, bf16[32,584,128]{2,1,0:T(8,128)(2,1)}, u32[]{:S(2)}) copy-start(bf16[32,584,128]{2,1,0:T(8,128)(2,1)} %copy-done) | copy-start | bytes 14352388

commit v2 on v1

v2 whole, which is shorter than its diff:
```python
import functools

import jax
import jax.numpy as jnp
from jax import lax
from jax.experimental import pallas as pl
from jax.experimental.pallas import tpu as pltpu
from jax.sharding import Mesh
from jax.sharding import PartitionSpec as P

STEPS = 2
USERS = ("users_0", "users_1", "users_2")
USERS_CAMPS = ("users_0", "users_1", "users_2", "camps")
TILE = 128
FLAGS = 8
GROUP = 8
HOT = 3
ACT = 32

VMEM = pl.BlockSpec(memory_space=pltpu.VMEM)
SMEM = pl.BlockSpec(memory_space=pltpu.SMEM)
HBM = pl.BlockSpec(memory_space=pl.ANY)


def pack_kernel(owned, ids_hbm, counts_hbm, scores_hbm, act_hbm, out_ref, ids, counts, scores, act, sems):
    copies = [
        pltpu.make_async_copy(src, dst, sems.at[n])
        for n, (src, dst) in enumerate(
            ((ids_hbm, ids), (counts_hbm, counts), (act_hbm, act), (scores_hbm, scores))
        )
    ]
    for copy in copies:
        copy.start()
    devices = out_ref.shape[0]
    hours = act.shape[0]
    blocks, slots = scores.shape[0], scores.shape[2]
    acts = blocks * owned * TILE
    flags = acts + blocks * hours
    lane = lax.broadcasted_iota(jnp.int32, (FLAGS, TILE), 1)
    for dev in range(devices):
        out_ref[dev, flags : flags + FLAGS, :] = jnp.zeros((FLAGS, TILE), jnp.bfloat16)
    copies[2].wait()
    for b in range(blocks):
        own = act[:, b * TILE : (b + 1) * TILE]
        for dev in range(devices):
            out_ref[dev, acts + b * hours : acts + (b + 1) * hours, :] = own
    copies[0].wait()
    copies[1].wait()
    copies[3].wait()
    for b in range(blocks):

        @pl.loop(0, jnp.minimum(counts[b], slots))
        def _(k):
            where = ids[b, 0, k]
            dev = where // owned
            slot = b * owned + lax.rem(where, owned)
            row = pl.multiple_of(slot * TILE, TILE)
            out_ref[dev, pl.ds(row, TILE), :] = scores[b, 0, k] * jnp.bfloat16(0.5)
            mark = jnp.where(lane == slot, 1.0, 0.0).astype(jnp.bfloat16)
            out_ref[dev, flags : flags + FLAGS, :] += mark


def collect(hours, owned, blocks, flags_ref, packets_ref, counts_ref, tiles, acts, far_tiles, far_acts, order, near, sems):
    devices = packets_ref.shape[0]
    act_rows = blocks * owned * TILE
    first = GROUP * HOT
    hour = lax.broadcasted_iota(jnp.int32, (ACT - hours, TILE), 0)
    tail = jnp.where(hour == 0, 1.0, 0.0).astype(jnp.bfloat16)
    counts = []
    for t in range(owned):
        n = jnp.int32(0)
        for i in range(devices):
            for b in range(blocks):
                order[t, n] = i * blocks + b
                n = n + flags_ref[i, b * owned + t]
        counts.append(n)
        counts_ref[t] = n
    most = functools.reduce(jnp.maximum, counts)
    full = jnp.minimum((most + GROUP - 1) // GROUP, HOT) * GROUP

    def lines(t, p):
        entry = order[t, p]
        dev = entry // blocks
        b = lax.rem(entry, blocks)
        row = pl.multiple_of((b * owned + t) * TILE, TILE)
        act_row = pl.multiple_of(act_rows + b * hours, 8)
        tile = packets_ref[dev, pl.ds(row, TILE), :]
        act = packets_ref[dev, pl.ds(act_row, hours), :]
        return tile, jnp.concatenate([act, tail], axis=0)

    def keep(t, p, tile, act):
        g, at = p // GROUP, pl.multiple_of(lax.rem(p, GROUP) * TILE, TILE)
        tiles[t, g, pl.ds(at, TILE), :] = tile
        acts[t, g, :, pl.ds(at, TILE)] = act

    for t in range(owned):

        @pl.loop(0, jnp.minimum(counts[t], first))
        def _(p, t=t):
            keep(t, p, *lines(t, p))

        @pl.loop(jnp.minimum(counts[t], first), full)
        def _(p, t=t):
            keep(t, p, jnp.zeros((TILE, TILE), jnp.bfloat16), jnp.zeros((ACT, TILE), jnp.bfloat16))

        @pl.loop(first, counts[t])
        def _(p, t=t):
            tile, act = lines(t, p)
            near[:TILE] = tile
            near[TILE:] = act
            for n, (src, dst) in enumerate(((near.at[:TILE], far_tiles), (near.at[TILE:], far_acts))):
                copy = pltpu.make_async_copy(src, dst.at[t, p - first], sems.at[n])
                copy.start()
                copy.wait()


def local_usage(owned, lam, counts_ref, tiles, acts, far_tiles, far_acts, near, sems):
    hours = lam.shape[0]
    first = GROUP * HOT
    hour = lax.broadcasted_iota(jnp.int32, (ACT - hours, TILE), 0)
    half = jnp.where(hour == 0, 0.5, 0.0).astype(jnp.bfloat16)
    weights = []
    for t in range(owned):
        rounded = lam[:, t * TILE : (t + 1) * TILE].astype(jnp.bfloat16)
        weights.append(jnp.concatenate([rounded * jnp.bfloat16(-0.5), half], axis=0))
    most = functools.reduce(jnp.maximum, [counts_ref[t] for t in range(owned)])

    def used(t, tile, act):
        part = lax.dot_general(
            act, weights[t], (((0,), (0,)), ((), ())), preferred_element_type=jnp.float32
        )
        share = jnp.clip(tile.astype(jnp.float32) + part, 0.0, 1.0).astype(jnp.bfloat16)
        return jnp.dot(act, share, preferred_element_type=jnp.float32)

    def group(g, totals):
        return tuple(totals[t] + used(t, tiles[t, g], acts[t, g]) for t in range(owned))

    def further(t, p, total):
        for n, (src, dst) in enumerate(((far_tiles, near.at[:TILE]), (far_acts, near.at[TILE:]))):
            copy = pltpu.make_async_copy(src.at[t, p - first], dst, sems.at[n])
            copy.start()
            copy.wait()
        return total + used(t, near[:TILE], near[TILE:])

    zeros = tuple(jnp.zeros((ACT, TILE), jnp.float32) for _ in range(owned))
    groups = jnp.minimum((most + GROUP - 1) // GROUP, HOT)
    totals = lax.fori_loop(0, groups, group, zeros)
    totals = [
        lax.fori_loop(first, jnp.maximum(counts_ref[t], first), functools.partial(further, t), totals[t])
        for t in range(owned)
    ]
    return jnp.concatenate([total[:hours] for total in totals], axis=1)


def scale_of(parts_ref, entries):
    squares = jnp.sum(jnp.sum(parts_ref[:, 0, :], axis=0, keepdims=True), axis=1, keepdims=True)
    return lax.rsqrt(squares / entries + 1e-06)


def moved(lam, gap, scale):
    return jnp.maximum(lam + 0.3 * (gap * scale), 0.0)


def direction_kernel(owned, blocks, entries, kind, *refs):
    if kind == "first":
        flags_ref, packets_ref, limit_ref, lam_ref, gap_ref, parts_ref, counts_ref = refs[:7]
        store = refs[7:11]
        near, sems, order = refs[11:]
        at = lam_ref[...]
        collect(at.shape[0], owned, blocks, flags_ref, packets_ref, counts_ref, *store, order, near, sems)
    else:
        counts_ref, store, limit_ref = refs[0], refs[1:5], refs[5]
        near, sems = refs[-2:]
        refs = refs[6:-2]
        if kind == "middle":
            lam_ref, before_ref, sums_ref, gap_ref, parts_ref = refs
            at = moved(lam_ref[...], before_ref[...], scale_of(sums_ref, entries))
        else:
            anchor_ref, lam_ref, before_ref, sums_ref, gap_ref, parts_ref, lam_out_ref = refs
            extra = moved(lam_ref[...], before_ref[...], scale_of(sums_ref, entries))
            weight = 1.0 / (kind + 2.0)
            at = weight * anchor_ref[...] + (1.0 - weight) * extra
            lam_out_ref[...] = at
    gap = local_usage(owned, at, counts_ref, *store, near, sems) - limit_ref[...]
    gap_ref[...] = gap
    squares = gap * gap
    line = sum(squares[:, t * TILE : (t + 1) * TILE] for t in range(owned))
    line = jnp.sum(line, axis=0, keepdims=True)
    parts_ref[...] = jnp.broadcast_to(line[None], parts_ref.shape)


def fold_kernel(parts_ref, out_ref):
    line = jnp.sum(parts_ref[:, 0, :], axis=0, keepdims=True)
    out_ref[...] = jnp.broadcast_to(line[None], out_ref.shape)


def final_kernel(entries, step, anchor_ref, lam_ref, gap_ref, sums_ref, new_ref, dir_ref):
    scale = scale_of(sums_ref, entries)
    gap = gap_ref[...]
    dir_ref[...] = gap * scale
    extra = moved(lam_ref[...], gap, scale)
    weight = 1.0 / (step + 2.0)
    new_ref[...] = weight * anchor_ref[...] + (1.0 - weight) * extra


def swapped(parts, axis):
    return lax.all_to_all(parts, axis, split_axis=0, concat_axis=0, tiled=True)


def on_device(scores, elig_ids, elig_counts, activity, prices, spend_limit):
    devices = lax.axis_size(USERS)
    groups = lax.axis_size("camps")
    entries = float(prices.size * devices * groups)
    hours, piece = prices.shape
    owned = piece // TILE
    blocks = scores.shape[0]
    rows = blocks * owned * TILE + blocks * hours + FLAGS
    far = max(devices * blocks - GROUP * HOT, 1)
    params = pltpu.CompilerParams(vmem_limit_bytes=8 * 2**20)

    packets = pl.pallas_call(
        functools.partial(pack_kernel, owned),
        out_shape=jax.ShapeDtypeStruct((devices, rows, TILE), jnp.bfloat16),
        in_specs=[HBM] * 4,
        out_specs=VMEM,
        scratch_shapes=[
            pltpu.SMEM(elig_ids.shape, jnp.int32),
            pltpu.SMEM((blocks,), jnp.int32),
            pltpu.VMEM(scores.shape, jnp.bfloat16),
            pltpu.VMEM(activity.shape, jnp.bfloat16),
            pltpu.SemaphoreType.DMA((4,)),
        ],
        compiler_params=params,
        name="pack",
    )(elig_ids, elig_counts[:, 0], scores, activity)
    packets = swapped(packets, USERS)
    flags = packets[:, rows - FLAGS, : blocks * owned].astype(jnp.int32)

    value = jax.ShapeDtypeStruct(prices.shape, jnp.float32)
    parts = jax.ShapeDtypeStruct((devices, 1, TILE), jnp.float32)
    scratch = [pltpu.VMEM((TILE + ACT, TILE), jnp.bfloat16), pltpu.SemaphoreType.DMA((2,))]
    store_shapes = [
        jax.ShapeDtypeStruct((owned, HOT, GROUP * TILE, TILE), jnp.bfloat16),
        jax.ShapeDtypeStruct((owned, HOT, ACT, GROUP * TILE), jnp.bfloat16),
        jax.ShapeDtypeStruct((owned, far, TILE, TILE), jnp.bfloat16),
        jax.ShapeDtypeStruct((owned, far, ACT, TILE), jnp.bfloat16),
    ]
    store_specs = [VMEM, VMEM, HBM, HBM]

    def total_of(part):
        over_users = pl.pallas_call(
            fold_kernel,
            out_shape=jax.ShapeDtypeStruct((groups, 1, TILE), jnp.float32),
            in_specs=[VMEM],
            out_specs=VMEM,
            compiler_params=params,
            name="fold",
        )(swapped(part, USERS))
        return swapped(over_users, "camps")

    def call(kind, ins, outs, in_specs, out_specs, scratch_shapes):
        return pl.pallas_call(
            functools.partial(direction_kernel, owned, blocks, entries, kind),
            out_shape=outs,
            in_specs=in_specs,
            out_specs=out_specs,
            scratch_shapes=scratch_shapes,
            compiler_params=params,
            name="direction",
        )(*ins)

    got = call(
        "first",
        (flags, packets, spend_limit, prices),
        [value, parts, jax.ShapeDtypeStruct((owned,), jnp.int32)] + store_shapes,
        [SMEM] + [VMEM] * 3,
        [VMEM, VMEM, SMEM] + store_specs,
        scratch + [pltpu.SMEM((owned, devices * blocks), jnp.int32)],
    )
    gap, sums, kept = got[0], total_of(got[1]), got[2:]

    def direction(kind, *args):
        outs = [value, parts] + ([value] if kind != "middle" else [])
        got = call(
            kind,
            (*kept, spend_limit, *args),
            outs,
            [SMEM] + store_specs + [VMEM] * (len(args) + 1),
            [VMEM] * len(outs),
            scratch,
        )
        return got[0], total_of(got[1]), got[2:]

    lam = prices
    for step in range(STEPS):
        gap, sums, _ = direction("middle", lam, gap, sums)
        if step < STEPS - 1:
            gap, sums, (lam,) = direction(step, prices, lam, gap, sums)
    new, last = pl.pallas_call(
        functools.partial(final_kernel, entries, STEPS - 1),
        out_shape=[value, value],
        in_specs=[VMEM] * 4,
        out_specs=[VMEM] * 2,
        compiler_params=params,
        name="final",
    )(prices, lam, gap, sums)
    return (new, last)


def solution(mesh):
    torus = Mesh(
        mesh.devices.reshape(4, 4, 2, mesh.shape["camps"]),
        ("users_0", "users_1", "users_2", "camps"),
    )
    in_specs = (
        P(USERS, "camps", None, None, None),
        P(USERS, "camps", None),
        P(USERS, "camps"),
        P(None, USERS),
        P(None, USERS_CAMPS),
        P(None, USERS_CAMPS),
    )
    out_specs = (P(None, USERS_CAMPS), P(None, USERS_CAMPS))
    return jax.shard_map(
        on_device, mesh=torus, in_specs=in_specs, out_specs=out_specs, check_vma=False
    )
```

time: 207 us -> 194 us (0.937)
  local copies, waits for them, and re-layouts: 12.4 us -> 3.18 us
  Pallas kernels: 13.6 us -> 8.45 us
    unnamed x20 -> x12, local copies, waits for them, and re-layouts: 12.4 us -> 3.18 us
    pallas_call x5 -> x8, Pallas kernels: 11.9 us -> 7.04 us  [the longest x4 6.93 us: call(): pl.pallas_call(functools.partial(direction_kernel, owned, blocks, entries...]
where the time goes in v2:
time: 194 us
  blocking collectives  181 us (93%)
  Pallas kernels  8.45 us (4%)
  local copies, waits for them, and re-layouts  3.18 us (2%)
    all_to_all x9, blocking collectives, swapped(): return lax.all_to_all(parts, axis, split_axis=0, concat_axis=0, tiled=True)  181 us
    pallas_call x4, Pallas kernels, call(): pl.pallas_call(functools.partial(direction_kernel, owned, blocks, entries...  6.93 us

profile of v2, /device:TPU:1, one launch (start us, length us, event | category | flops | bytes accessed | tf_op | source)
XLA Modules:
  0.0 193.6 jit_solution(581899627985568325)
XLA Ops:
  0.6 0.0 copy-start
  0.6 1.1 copy-done
  1.8 0.0 copy-start.3
  1.8 0.7 copy-done.3
  2.5 0.0 copy-start.4
  2.5 0.7 copy-done.4
  3.2 0.0 copy-start.5
  3.2 0.7 copy-done.5
  3.8 0.7 pack.1
  4.5 0.0 copy-start.1
  4.5 0.0 copy-start.2
  4.5 65.6 %all_to_all.45.refs_1_ = bf16[32,568,128]{2,1,0:T(8,128)(2,1)S(1)} all-to-all(bf16[32,568,128]{2,1,0:T(8,128)(2,1)S(1)} %pack.1), channel_id=1, replica_groups=mesh['users_0'=4,'users_1'=4,'users_2'=2,'camps'=16] {'users_0','users_1..., dimensions={0} | all-to-all | bytes 9306112 | tf_op jit(solution)/shard_map/all_to_all | solution.py:207
  70.2 0.0 copy-done.1
  70.2 0.0 copy-done.2
  70.2 2.8 %direction.4 = (f32[24,256]{1,0:T(8,128)S(1)}, f32[32,1,128]{2,1,0:T(1,128)S(1)}, s32[2]{0:T(128)S(1)}, bf16[2,3,1024,128]{3,2,1,0:T(8,128)(2,1)S(1)}, bf16[2,3,...) custom-call(s32[32,4]{1,0:T(8,128)S(1)} %bitcast.2, ...), custom_call_target="tpu_custom_call" | custom-call | tf_op jit(solution)/shard_map/direction/pallas_call | solution.py:262
  72.9 12.0 %all_to_all.46.parts_ref = f32[32,1,128]{2,1,0:T(1,128)S(1)} all-to-all(f32[32,1,128]{2,1,0:T(1,128)S(1)} %get-tuple-element.22), channel_id=1, replica_groups=mesh['users_0'=4,'users_1'=4,'users_2'=2,'camps'=16] {'users_0','users_1..., dimensions={0} | all-to-all | bytes 32768 | tf_op jit(solution)/shard_map/all_to_all | solution.py:207
  84.9 24.3 %all_to_all.47.refs_8_ = f32[16,1,128]{2,1,0:T(1,128)S(1)} all-to-all(f32[16,1,128]{2,1,0:T(1,128)S(1)} %fold.4), channel_id=1, replica_groups=mesh['users_0'=4,'users_1'=4,'users_2'=2,'camps'=16] {'camps'}, dimensions={0} | all-to-all | bytes 16384 | tf_op jit(solution)/shard_map/all_to_all | solution.py:207
  109.2 1.4 direction.5
  110.6 12.8 %all_to_all.48.parts_ref = f32[32,1,128]{2,1,0:T(1,128)S(1)} all-to-all(f32[32,1,128]{2,1,0:T(1,128)S(1)} %get-tuple-element.24), channel_id=1, replica_groups=mesh['users_0'=4,'users_1'=4,'users_2'=2,'camps'=16] {'users_0','users_1..., dimensions={0} | all-to-all | bytes 32768 | tf_op jit(solution)/shard_map/all_to_all | solution.py:207
  123.4 13.8 %all_to_all.49.refs_9_ = f32[16,1,128]{2,1,0:T(1,128)S(1)} all-to-all(f32[16,1,128]{2,1,0:T(1,128)S(1)} %fold.5), channel_id=1, replica_groups=mesh['users_0'=4,'users_1'=4,'users_2'=2,'camps'=16] {'camps'}, dimensions={0} | all-to-all | bytes 16384 | tf_op jit(solution)/shard_map/all_to_all | solution.py:207
  137.3 1.4 direction.6
  138.7 12.5 %all_to_all.50.parts_ref = f32[32,1,128]{2,1,0:T(1,128)S(1)} all-to-all(f32[32,1,128]{2,1,0:T(1,128)S(1)} %get-tuple-element.27), channel_id=1, replica_groups=mesh['users_0'=4,'users_1'=4,'users_2'=2,'camps'=16] {'users_0','users_1..., dimensions={0} | all-to-all | bytes 32768 | tf_op jit(solution)/shard_map/all_to_all | solution.py:207
  151.2 13.8 %all_to_all.51.refs_8_ = f32[16,1,128]{2,1,0:T(1,128)S(1)} all-to-all(f32[16,1,128]{2,1,0:T(1,128)S(1)} %fold.6), channel_id=1, replica_groups=mesh['users_0'=4,'users_1'=4,'users_2'=2,'camps'=16] {'camps'}, dimensions={0} | all-to-all | bytes 16384 | tf_op jit(solution)/shard_map/all_to_all | solution.py:207
  165.1 1.4 direction.7
  166.5 12.5 %all_to_all.52.parts_ref = f32[32,1,128]{2,1,0:T(1,128)S(1)} all-to-all(f32[32,1,128]{2,1,0:T(1,128)S(1)} %get-tuple-element.29), channel_id=1, replica_groups=mesh['users_0'=4,'users_1'=4,'users_2'=2,'camps'=16] {'users_0','users_1..., dimensions={0} | all-to-all | bytes 32768 | tf_op jit(solution)/shard_map/all_to_all | solution.py:207
  179.0 13.8 %all_to_all.53.sums_ref = f32[16,1,128]{2,1,0:T(1,128)S(1)} all-to-all(f32[16,1,128]{2,1,0:T(1,128)S(1)} %fold.7), channel_id=1, replica_groups=mesh['users_0'=4,'users_1'=4,'users_2'=2,'camps'=16] {'camps'}, dimensions={0} | all-to-all | bytes 16384 | tf_op jit(solution)/shard_map/all_to_all | solution.py:207
  192.9 0.7 final.1
  (5 shorter events, 0.1 us)
Async XLA Ops:
  0.6 1.1 copy-start
  1.8 0.7 copy-start.3
  2.5 0.7 copy-start.4
  3.2 0.7 copy-start.5
  4.5 65.7 %copy-start.1 = (f32[24,256]{1,0:T(8,128)S(1)}, f32[24,256]{1,0:T(8,128)}, u32[]{:S(2)}) copy-start(f32[24,256]{1,0:T(8,128)} %anchor_ref.1) | copy-start | bytes 73732
  4.5 65.7 %copy-start.2 = (f32[24,256]{1,0:T(8,128)S(1)}, f32[24,256]{1,0:T(8,128)}, u32[]{:S(2)}) copy-start(f32[24,256]{1,0:T(8,128)} %refs_5_.5) | copy-start | bytes 73732

commit v3 on v2

v3 whole, which is shorter than its diff:
```python
import functools

import jax
import jax.numpy as jnp
from jax import lax
from jax.experimental import pallas as pl
from jax.experimental.pallas import tpu as pltpu
from jax.sharding import Mesh
from jax.sharding import PartitionSpec as P

STEPS = 2
USERS = ("users_0", "users_1", "users_2")
USERS_CAMPS = ("users_0", "users_1", "users_2", "camps")
TILE = 128
LINES = 8
LIST = 19
GROUP = 8
ACT = 32

VMEM = pl.BlockSpec(memory_space=pltpu.VMEM)
SMEM = pl.BlockSpec(memory_space=pltpu.SMEM)
HBM = pl.BlockSpec(memory_space=pltpu.HBM)
PARAMS = pltpu.CompilerParams(vmem_limit_bytes=8 * 2**20)


def copied(src, dst, sem):
    copy = pltpu.make_async_copy(src, dst, sem)
    copy.start()
    copy.wait()


def cut_kernel(ids_ref, scores_hbm, act_hbm, out_ref, scores, act, sems):
    load_act = pltpu.make_async_copy(act_hbm, act, sems.at[0])
    load_scores = pltpu.make_async_copy(scores_hbm, scores, sems.at[1])
    load_act.start()
    load_scores.start()
    devices = out_ref.shape[0]
    hours = act.shape[0]
    blocks, slots = scores.shape[0], scores.shape[2]
    piece = TILE * blocks // devices
    acts = slots * piece
    lines = acts + blocks * hours
    ids = ids_ref[...]
    for dev in range(devices):
        out_ref[dev, lines : lines + LINES, :] = ids
    load_act.wait()
    for b in range(blocks):
        own = act[:, b * TILE : (b + 1) * TILE]
        for dev in range(devices):
            out_ref[dev, acts + b * hours : acts + (b + 1) * hours, :] = own
    load_scores.wait()
    for b in range(blocks):
        for k in range(slots):
            for q in range(devices // blocks):
                rows = scores[b, 0, k, q * piece : (q + 1) * piece, :] * jnp.bfloat16(0.5)
                out_ref[q * blocks + b, k * piece : (k + 1) * piece, :] = rows


def route_kernel(owned, slots, which_ref, *refs):
    ids_refs, packets_ref = refs[:-8], refs[-8]
    out_ref, longest_ref = refs[-7:-5]
    places, where, sem = refs[-3:]
    blocks = len(ids_refs)
    devices = packets_ref.shape[0]
    piece = TILE * blocks // devices
    shape = (devices, TILE)
    lane = lax.broadcasted_iota(jnp.int32, shape, 1)
    source = lax.broadcasted_iota(jnp.int32, (devices, 1), 0)
    which = which_ref[0]

    def owner_is(ids, k):
        column = ids[:, k : k + 1]
        return column, jnp.where(column < 0, -1, column // owned) == lane

    longest = jnp.float32(0.0)
    for ids_ref in ids_refs:
        held = jnp.zeros(shape, jnp.float32)
        for k in range(slots):
            held += owner_is(ids_ref[...], k)[1].astype(jnp.float32)
        longest = jnp.maximum(longest, jnp.max(jnp.sum(held, axis=0, keepdims=True)))
    longest_ref[0] = longest.astype(jnp.int32)

    mine = ids_refs[0][...]
    for b in range(1, blocks):
        mine = jnp.where(which == b, ids_refs[b][...], mine)
    held = jnp.zeros(shape, jnp.float32)
    hits = []
    for k in range(slots):
        column, hit = owner_is(mine, k)
        hits.append((column, hit.astype(jnp.float32)))
        held += hits[-1][1]
    row = lax.broadcasted_iota(jnp.int32, (devices, devices), 0)
    col = lax.broadcasted_iota(jnp.int32, (devices, devices), 1)
    before = jnp.where(col < row, 1.0, 0.0).astype(jnp.bfloat16)
    ranks = jnp.dot(before, held.astype(jnp.bfloat16), preferred_element_type=jnp.float32)
    place = jnp.zeros(shape, jnp.int32)
    notes = jnp.zeros((TILE, TILE), jnp.float32)
    for k in range(slots):
        column, hit = hits[k]
        rank = jnp.sum(hit * ranks, axis=1, keepdims=True).astype(jnp.int32)
        ranks += hit
        live = jnp.logical_and(column >= 0, rank < LIST)
        spot = jnp.where(live, column // owned * (LIST + 1) + rank, LIST)
        place = jnp.where(lane == k, spot, place)
        code = (source * owned + lax.rem(column, owned) + 1).astype(jnp.float32)
        note = jnp.where(jnp.logical_and(lane == rank, live), code, 0.0)
        notes += lax.dot_general(
            hit.astype(jnp.bfloat16),
            note.astype(jnp.bfloat16),
            (((0,), (0,)), ((), ())),
            preferred_element_type=jnp.float32,
        )
    places[...] = place
    copied(places, where, sem)

    @pl.loop(0, devices)
    def _(i):
        for k in range(slots):
            out_ref[where[i, k]] = packets_ref[i, k * piece : (k + 1) * piece, :]

    for j in range(devices):
        note = jnp.broadcast_to(notes[j : j + 1, :], (piece, TILE))
        out_ref[j * (LIST + 1) + LIST] = note.astype(jnp.bfloat16)


def pack_kernel(owned, ids, counts, scores, act, out_ref):
    devices = out_ref.shape[0]
    hours = act.shape[0]
    blocks, slots = scores.shape[0], scores.shape[2]
    acts = blocks * owned * TILE
    flags = acts + blocks * hours
    lane = lax.broadcasted_iota(jnp.int32, (LINES, TILE), 1)

    @pl.loop(0, devices)
    def _(dev):
        out_ref[dev, flags : flags + LINES, :] = jnp.zeros((LINES, TILE), jnp.bfloat16)
        for b in range(blocks):
            own = act[:, b * TILE : (b + 1) * TILE]
            out_ref[dev, acts + b * hours : acts + (b + 1) * hours, :] = own

    for b in range(blocks):

        @pl.loop(0, jnp.minimum(counts[b], slots))
        def _(k):
            at = ids[b, 0, k]
            dev = at // owned
            slot = b * owned + lax.rem(at, owned)
            row = pl.multiple_of(slot * TILE, TILE)
            out_ref[dev, pl.ds(row, TILE), :] = scores[b, 0, k] * jnp.bfloat16(0.5)
            mark = jnp.where(lane == slot, (k + 1).astype(jnp.float32), 0.0)
            out_ref[dev, flags : flags + LINES, :] += mark.astype(jnp.bfloat16)


def activity_rows(act):
    hour = lax.broadcasted_iota(jnp.int32, (ACT - act.shape[0], TILE), 0)
    return jnp.concatenate([act, jnp.where(hour == 0, 1.0, 0.0).astype(jnp.bfloat16)], axis=0)


def far_kernel(hours, owned, blocks, flags_ref, packets_ref, far_tiles, far_acts, counts_ref, near, sem):
    devices = packets_ref.shape[0]
    acts = blocks * owned * TILE
    for t in range(owned):
        counts_ref[t] = 0
    for b in range(blocks):

        @pl.loop(0, devices, init_carry=jnp.int32(0))
        def _(i, taken, b=b):
            flags = [flags_ref[i, b * owned + t] for t in range(owned)]
            for t in range(owned):
                rank = taken
                for flag in flags:
                    rank += jnp.logical_and(flag > 0, flag < flags[t]).astype(jnp.int32)

                @pl.when(jnp.logical_and(flags[t] > 0, rank >= LIST))
                def _(t=t):
                    n = counts_ref[t]
                    slot = b * owned + t
                    near[:TILE] = packets_ref[i, slot * TILE : (slot + 1) * TILE, :]
                    rows = packets_ref[i, acts + b * hours : acts + (b + 1) * hours, :]
                    near[TILE:] = activity_rows(rows)
                    copied(near.at[:TILE], far_tiles.at[t, n], sem)
                    copied(near.at[TILE:], far_acts.at[t, n], sem)
                    counts_ref[t] = n + 1

            return taken + sum((flag > 0).astype(jnp.int32) for flag in flags)


def collect(hours, owned, blocks, notes_ref, far_counts_ref, packets_ref, lists_ref, counts_ref, tiles, acts, order):
    devices = packets_ref.shape[0]
    piece = TILE * blocks // devices
    act_rows = packets_ref.shape[1] - LINES - blocks * hours
    counts = [jnp.int32(0)] * owned
    for b in range(blocks):
        for r in range(LIST):
            code = notes_ref[b, r] - 1
            live = (code >= 0).astype(jnp.int32)
            code = jnp.maximum(code, 0)
            block = lax.rem(code, owned)
            entry = (code // owned * blocks + b) * LIST + r
            for t in range(owned):
                order[t, counts[t]] = entry
                counts[t] += live * (block == t).astype(jnp.int32)
    for t in range(owned):
        counts_ref[t] = counts[t]
        counts_ref[owned + t] = far_counts_ref[t]
    most = functools.reduce(jnp.maximum, counts)
    full = (most + GROUP - 1) // GROUP * GROUP

    for t in range(owned):

        @pl.loop(0, counts[t])
        def _(p, t=t):
            entry = order[t, p]
            r = lax.rem(entry, LIST)
            pair = entry // LIST
            dev = pair // blocks
            b = lax.rem(pair, blocks)
            g, at = p // GROUP, pl.multiple_of(lax.rem(p, GROUP) * TILE, TILE)
            for q in range(devices // blocks):
                rows = lists_ref[(q * blocks + b) * (LIST + 1) + r]
                tiles[t, g, pl.ds(at + q * piece, piece), :] = rows
            act_row = pl.multiple_of(act_rows + b * hours, 8)
            acts[t, g, :, pl.ds(at, TILE)] = activity_rows(packets_ref[dev, pl.ds(act_row, hours), :])

        @pl.loop(counts[t], full)
        def _(p, t=t):
            g, at = p // GROUP, pl.multiple_of(lax.rem(p, GROUP) * TILE, TILE)
            tiles[t, g, pl.ds(at, TILE), :] = jnp.zeros((TILE, TILE), jnp.bfloat16)
            acts[t, g, :, pl.ds(at, TILE)] = jnp.zeros((ACT, TILE), jnp.bfloat16)


def local_usage(owned, lam, counts_ref, tiles, acts, far_tiles, far_acts, near, sem):
    hours = lam.shape[0]
    hour = lax.broadcasted_iota(jnp.int32, (ACT - hours, TILE), 0)
    half = jnp.where(hour == 0, 0.5, 0.0).astype(jnp.bfloat16)
    weights = []
    for t in range(owned):
        rounded = lam[:, t * TILE : (t + 1) * TILE].astype(jnp.bfloat16)
        weights.append(jnp.concatenate([rounded * jnp.bfloat16(-0.5), half], axis=0))
    most = functools.reduce(jnp.maximum, [counts_ref[t] for t in range(owned)])

    def used(t, tile, act):
        part = lax.dot_general(
            act, weights[t], (((0,), (0,)), ((), ())), preferred_element_type=jnp.float32
        )
        share = jnp.clip(tile.astype(jnp.float32) + part, 0.0, 1.0).astype(jnp.bfloat16)
        return jnp.dot(act, share, preferred_element_type=jnp.float32)

    def group(g, totals):
        return tuple(totals[t] + used(t, tiles[t, g], acts[t, g]) for t in range(owned))

    def further(t, p, total):
        copied(far_tiles.at[t, p], near.at[:TILE], sem)
        copied(far_acts.at[t, p], near.at[TILE:], sem)
        return total + used(t, near[:TILE], near[TILE:])

    zeros = tuple(jnp.zeros((ACT, TILE), jnp.float32) for _ in range(owned))
    totals = lax.fori_loop(0, (most + GROUP - 1) // GROUP, group, zeros)
    totals = [
        lax.fori_loop(0, counts_ref[owned + t], functools.partial(further, t), totals[t])
        for t in range(owned)
    ]
    return jnp.concatenate([total[:hours] for total in totals], axis=1)


def scale_of(parts_ref, entries):
    squares = jnp.sum(jnp.sum(parts_ref[:, 0, :], axis=0, keepdims=True), axis=1, keepdims=True)
    return lax.rsqrt(squares / entries + 1e-06)


def moved(lam, gap, scale):
    return jnp.maximum(lam + 0.3 * (gap * scale), 0.0)


def direction_kernel(owned, blocks, entries, kind, *refs):
    if kind == "first":
        far, (notes_ref, far_counts_ref, packets_ref, lists_ref, limit_ref, lam_ref) = refs[:2], refs[2:8]
        gap_ref, parts_ref, counts_ref = refs[8:11]
        store = refs[11:13]
        near, sem, order = refs[13:]
        at = lam_ref[...]
        collect(
            at.shape[0], owned, blocks, notes_ref, far_counts_ref, packets_ref, lists_ref, counts_ref, *store, order
        )
    else:
        far, counts_ref, store, limit_ref = refs[:2], refs[2], refs[3:5], refs[5]
        near, sem = refs[-2:]
        refs = refs[6:-2]
        if kind == "middle":
            lam_ref, before_ref, sums_ref, gap_ref, parts_ref = refs
            at = moved(lam_ref[...], before_ref[...], scale_of(sums_ref, entries))
        else:
            anchor_ref, lam_ref, before_ref, sums_ref, gap_ref, parts_ref, lam_out_ref = refs
            extra = moved(lam_ref[...], before_ref[...], scale_of(sums_ref, entries))
            weight = 1.0 / (kind + 2.0)
            at = weight * anchor_ref[...] + (1.0 - weight) * extra
            lam_out_ref[...] = at
    gap = local_usage(owned, at, counts_ref, *store, *far, near, sem) - limit_ref[...]
    gap_ref[...] = gap
    squares = gap * gap
    line = sum(squares[:, t * TILE : (t + 1) * TILE] for t in range(owned))
    line = jnp.sum(line, axis=0, keepdims=True)
    parts_ref[...] = jnp.broadcast_to(line[None], parts_ref.shape)


def fold_kernel(parts_ref, out_ref):
    line = jnp.sum(parts_ref[:, 0, :], axis=0, keepdims=True)
    out_ref[...] = jnp.broadcast_to(line[None], out_ref.shape)


def final_kernel(entries, step, anchor_ref, lam_ref, gap_ref, sums_ref, new_ref, dir_ref):
    scale = scale_of(sums_ref, entries)
    gap = gap_ref[...]
    dir_ref[...] = gap * scale
    extra = moved(lam_ref[...], gap, scale)
    weight = 1.0 / (step + 2.0)
    new_ref[...] = weight * anchor_ref[...] + (1.0 - weight) * extra


def swapped(parts, axis):
    return lax.all_to_all(parts, axis, split_axis=0, concat_axis=0, tiled=True)


def kernel_call(body, name, out_shape, in_specs, out_specs, scratch_shapes=()):
    return pl.pallas_call(
        body,
        out_shape=out_shape,
        in_specs=in_specs,
        out_specs=out_specs,
        scratch_shapes=scratch_shapes,
        compiler_params=PARAMS,
        name=name,
    )


def on_device(scores, elig_ids, elig_counts, activity, prices, spend_limit):
    devices = lax.axis_size(USERS)
    groups = lax.axis_size("camps")
    entries = float(prices.size * devices * groups)
    hours, width = prices.shape
    owned = width // TILE
    blocks, slots = scores.shape[0], scores.shape[2]
    piece = TILE * blocks // devices
    act_rows = slots * piece
    lines = act_rows + blocks * hours
    bf16, f32, i32 = jnp.bfloat16, jnp.float32, jnp.int32
    shape = jax.ShapeDtypeStruct

    slot_ids = jnp.arange(slots, dtype=i32)
    ids = jnp.where(slot_ids[None, :] < elig_counts, elig_ids[:, 0], -1).astype(bf16)
    ids = jnp.pad(ids, ((0, LINES - blocks), (0, TILE - slots)), constant_values=-1)
    packets = kernel_call(
        cut_kernel,
        "cut",
        shape((devices, lines + LINES, TILE), bf16),
        [VMEM, HBM, HBM],
        VMEM,
        [
            pltpu.VMEM(scores.shape, bf16),
            pltpu.VMEM(activity.shape, bf16),
            pltpu.SemaphoreType.DMA((2,)),
        ],
    )(ids, scores, activity)
    packets = swapped(packets, USERS)

    which = lax.rem(lax.axis_index(USERS), blocks).astype(i32).reshape(1)
    far_slots = devices * blocks
    listed, longest, far_tiles, far_acts = kernel_call(
        functools.partial(route_kernel, owned, slots),
        "route",
        [
            shape((devices * (LIST + 1), piece, TILE), bf16),
            shape((1,), i32),
            shape((owned, far_slots, TILE, TILE), bf16),
            shape((owned, far_slots, ACT, TILE), bf16),
        ],
        [SMEM] + [VMEM] * (blocks + 1),
        [VMEM, SMEM, HBM, HBM],
        [
            pltpu.VMEM((devices, TILE), i32),
            pltpu.SMEM((devices, TILE), i32),
            pltpu.SemaphoreType.DMA,
        ],
    )(which, *(packets[:, lines + b].astype(i32) for b in range(blocks)), packets)
    near = pltpu.VMEM((TILE + ACT, TILE), bf16)

    def direct(carry):
        rows = blocks * owned * TILE + blocks * hours
        dense = kernel_call(
            functools.partial(pack_kernel, owned),
            "pack",
            shape((devices, rows + LINES, TILE), bf16),
            [SMEM, SMEM, VMEM, VMEM],
            VMEM,
        )(elig_ids, elig_counts[:, 0], scores, activity)
        dense = swapped(dense, USERS)
        flags = dense[:, rows, : blocks * owned].astype(i32)
        kept = kernel_call(
            functools.partial(far_kernel, hours, owned, blocks),
            "far",
            [shape(far_tiles.shape, bf16), shape(far_acts.shape, bf16), shape((owned,), i32)],
            [SMEM, VMEM],
            [HBM, HBM, SMEM],
            [near, pltpu.SemaphoreType.DMA],
        )(flags, dense)
        return (jnp.int32(0), *kept)

    _, far_tiles, far_acts, far_counts = lax.while_loop(
        lambda carry: carry[0] > LIST, direct, (longest[0], far_tiles, far_acts, jnp.zeros((owned,), i32))
    )
    far = (far_tiles, far_acts)
    listed = swapped(listed, USERS)
    notes = listed.reshape(devices, LIST + 1, piece, TILE)[:blocks, LIST, 0, :LIST].astype(i32)

    value = shape(prices.shape, f32)
    parts = shape((devices, 1, TILE), f32)
    scratch = [near, pltpu.SemaphoreType.DMA]
    full = pl.cdiv(blocks * LIST, GROUP)
    store_shapes = [
        shape((owned, full, GROUP * TILE, TILE), bf16),
        shape((owned, full, ACT, GROUP * TILE), bf16),
    ]

    def total_of(part):
        folded = kernel_call(fold_kernel, "fold", shape((groups, 1, TILE), f32), [VMEM], VMEM)(swapped(part, USERS))
        return swapped(folded, "camps")

    def body_of(kind):
        return functools.partial(direction_kernel, owned, blocks, entries, kind)

    got = kernel_call(
        body_of("first"),
        "direction",
        [value, parts, shape((2 * owned,), i32)] + store_shapes,
        [HBM, HBM, SMEM, SMEM] + [VMEM] * 4,
        [VMEM, VMEM, SMEM, VMEM, VMEM],
        scratch + [pltpu.SMEM((owned, blocks * LIST), i32)],
    )(*far, notes, far_counts, packets, listed, spend_limit, prices)
    gap, sums, kept = got[0], total_of(got[1]), got[2:]

    def direction(kind, *args):
        outs = [value, parts] + ([value] if kind != "middle" else [])
        got = kernel_call(
            body_of(kind),
            "direction",
            outs,
            [HBM, HBM, SMEM] + [VMEM] * (len(args) + 3),
            [VMEM] * len(outs),
            scratch,
        )(*far, *kept, spend_limit, *args)
        return got[0], total_of(got[1]), got[2:]

    lam = prices
    for step in range(STEPS):
        gap, sums, _ = direction("middle", lam, gap, sums)
        if step < STEPS - 1:
            gap, sums, (lam,) = direction(step, prices, lam, gap, sums)
    new, last = kernel_call(
        functools.partial(final_kernel, entries, STEPS - 1), "final", [value, value], [VMEM] * 4, [VMEM] * 2
    )(prices, lam, gap, sums)
    return (new, last)


def solution(mesh):
    torus = Mesh(
        mesh.devices.reshape(4, 4, 2, mesh.shape["camps"]),
        ("users_0", "users_1", "users_2", "camps"),
    )
    in_specs = (
        P(USERS, "camps", None, None, None),
        P(USERS, "camps", None),
        P(USERS, "camps"),
        P(None, USERS),
        P(None, USERS_CAMPS),
        P(None, USERS_CAMPS),
    )
    out_specs = (P(None, USERS_CAMPS), P(None, USERS_CAMPS))
    return jax.shard_map(
        on_device, mesh=torus, in_specs=in_specs, out_specs=out_specs, check_vma=False
    )
```

time: 194 us -> 186 us (0.959)
  blocking collectives: 181 us -> 136 us
  waiting for transfers between devices: 0 us -> 18.8 us
  starting transfers between devices: 0 us -> 10.4 us
  Pallas kernels: 8.45 us -> 17.5 us
  local copies, waits for them, and re-layouts: 3.18 us -> 0.61 us
    all_to_all x9, blocking collectives: 181 us -> 136 us  [swapped(): return lax.all_to_all(parts, axis, split_axis=0, concat_axis=0, tiled=True)]
    all_to_all x0 -> x1, waiting for transfers between devices: none -> 18.8 us  [swapped(): return lax.all_to_all(parts, axis, split_axis=0, concat_axis=0, tiled=True)]
    all_to_all x0 -> x1, starting transfers between devices: none -> 10.4 us  [swapped(): return lax.all_to_all(parts, axis, split_axis=0, concat_axis=0, tiled=True)]
    pallas_call x10 -> x11, Pallas kernels: 8.45 us -> 17.5 us  [the longest x3 6.24 us: direction(): kernel_call(body_of(kind), 'direction', outs, [HBM, HBM, SMEM] + [VMEM] *...]
    unnamed x12 -> x16, local copies, waits for them, and re-layouts: 3.18 us -> 0.08 us
  transfers between devices with their start and end apart: 0 -> 1, of which waited for: 0 -> 1; matrix products, arithmetic and copies ran while one was open for 0% -> 0% of each run, Pallas kernels for 0% -> 0%
where the time goes in v3:
time: 186 us
  blocking collectives  136 us (73%)
  waiting for transfers between devices  18.8 us (10%)
  Pallas kernels  17.5 us (9%)
  starting transfers between devices  10.4 us (6%)
    all_to_all x9, blocking collectives, swapped(): return lax.all_to_all(parts, axis, split_axis=0, concat_axis=0, tiled=True)  136 us
    all_to_all x1, waiting for transfers between devices, swapped(): return lax.all_to_all(parts, axis, split_axis=0, concat_axis=0, tiled=True)  18.8 us
    all_to_all x1, starting transfers between devices, swapped(): return lax.all_to_all(parts, axis, split_axis=0, concat_axis=0, tiled=True)  10.4 us
    pallas_call x3, Pallas kernels, direction(): kernel_call(body_of(kind), 'direction', outs, [HBM, HBM, SMEM] + [VMEM] *...  6.24 us
    pallas_call x1, Pallas kernels, on_device(): kernel_call(body_of('first'), 'direction', [value, parts, shape((2 * owne...  4.28 us
  transfers between devices with their start and end apart: 1, of which 1 were waited for; matrix products, arithmetic and copies ran while one was open for 0% of the time, Pallas kernels for 0%

profile of v3, /device:TPU:1, one launch (start us, length us, event | category | flops | bytes accessed | tf_op | source)
XLA Modules:
  0.0 185.6 jit_solution(6076640897733236736)
XLA Ops:
  0.6 0.8 fusion
  1.4 0.0 copy-start.4
  1.4 0.0 copy-start.6
  1.4 0.0 copy-start.7
  1.4 0.0 copy-start.8
  1.4 2.5 %cut.1 = bf16[32,152,128]{2,1,0:T(8,128)(2,1)} custom-call(bf16[8,128]{1,0:T(8,128)(2,1)S(1)} %pad.4.ids_ref, bf16[2,1,12,128,128]{4,3,2,1,0:T(8,128)(2,1)} %scores_hbm.1, bf16[24,256]{1,0:T(8,128)(2,1)} %act_hbm.1), custom_call_target="tpu_custom_call" | custom-call | tf_op jit(solution)/shard_map/cut/pallas_call | solution.py:352
  3.9 10.4 %all-to-all-start.1 = ((bf16[32,152,128]{2,1,0:T(8,128)(2,1)}), bf16[32,152,128]{2,1,0:T(8,128)(2,1)S(1)}, u32[]{:S(2)}, u32[]{:S(2)}) async-start(bf16[32,152,128]{2,1,0:T(8,128)(2,1)} %cut.1), calls=%async_computation.1 | async-start | bytes 2490368 | tf_op jit(solution)/shard_map/all_to_all | solution.py:321
  14.4 18.8 %all-to-all-done.1.refs_2_.refs_4_ = bf16[32,152,128]{2,1,0:T(8,128)(2,1)S(1)} async-done(((bf16[32,152,128]{2,1,0:T(8,128)(2,1)}), bf16[32,152,128]{2,1,0:T(8,128)(2,1)S(1)}, u32[]{:S(2)}, u32[]{:S(2)}) %all-to-all-start.1) | async-done | bytes 1245216 | tf_op jit(solution)/shard_map/all_to_all | solution.py:321
  33.3 3.6 %route.1 = (bf16[640,8,128]{2,1,0:T(8,128)(2,1)S(1)}, s32[1]{0:T(128)}, bf16[2,64,128,128]{3,2,1,0:T(8,128)(2,1)}, bf16[2,64,32,128]{3,2,1,0:T(8,128)(2,1)}) custom-call(s32[1]{0:T(128)} %bitcast.2.which_ref, s32[32,128]{1,0:T(8,128)S(1)} %bitcast.17, s32[32,128]{1,0:T(8,128)S(1)} %bitcast.16, bf16[32,152,128]{2,1,0:T(8,128)(2,1)S(1)} %all-to-all-done.1.refs_2_.refs_4_), custom_call_target="tpu_custom_call" | custom-call | tf_op jit(solution)/shard_map/route/pallas_call | solution.py:368
  36.9 24.1 %all_to_all.54.refs_5_ = bf16[640,8,128]{2,1,0:T(8,128)(2,1)S(1)} all-to-all(bf16[640,8,128]{2,1,0:T(8,128)(2,1)S(1)} %get-tuple-element.66), channel_id=1, replica_groups=mesh['users_0'=4,'users_1'=4,'users_2'=2,'camps'=16] {'users_0','users_1..., dimensions={0} | all-to-all | bytes 2621440 | tf_op jit(solution)/shard_map/all_to_all | solution.py:321
  61.0 0.5 broadcast.6
  61.5 0.0 copy-done.4
  61.5 0.0 copy-done.6
  61.5 0.0 copy-done.7
  61.5 0.0 copy-done.8
  61.5 0.0 copy-start.1
  61.5 0.0 copy-start.2
  61.6 0.7 while.13
  62.2 0.0 copy-start.3
  62.2 0.0 copy-start.5
  62.2 0.0 copy-done.1
  62.3 0.0 copy-done.2
  62.3 4.3 %direction.4 = (f32[24,256]{1,0:T(8,128)S(1)}, f32[32,1,128]{2,1,0:T(1,128)S(1)}, s32[4]{0:T(128)S(1)}, bf16[2,5,1024,128]{3,2,1,0:T(8,128)(2,1)S(1)}, bf16[2,5,32,1024]{3,2,1,0:T(8,128)(2,1)S(1)}) custom-call(bf16[2,64,128,128]{3,2,1,0:T(8,128)(2,1)} %get-tuple-element.64.refs_0_, bf16[2,64,32,128]{3,2,1,0:T(8,128)(2,1)} %get-tuple-element.65.refs_1_, ...), custom_call_target="tpu_custom_call" | custom-call | tf_op jit(solution)/shard_map/direction/pallas_call | solution.py:431
  66.6 10.4 %all_to_all.55.parts_ref = f32[32,1,128]{2,1,0:T(1,128)S(1)} all-to-all(f32[32,1,128]{2,1,0:T(1,128)S(1)} %get-tuple-element.72), channel_id=1, replica_groups=mesh['users_0'=4,'users_1'=4,'users_2'=2,'camps'=16] {'users_0','users_1..., dimensions={0} | all-to-all | bytes 32768 | tf_op jit(solution)/shard_map/all_to_all | solution.py:321
  77.0 24.3 %all_to_all.56.refs_8_ = f32[16,1,128]{2,1,0:T(1,128)S(1)} all-to-all(f32[16,1,128]{2,1,0:T(1,128)S(1)} %fold.4), channel_id=1, replica_groups=mesh['users_0'=4,'users_1'=4,'users_2'=2,'camps'=16] {'camps'}, dimensions={0} | all-to-all | bytes 16384 | tf_op jit(solution)/shard_map/all_to_all | solution.py:321
  101.3 0.0 copy-done.3
  101.3 0.0 copy-done.5
  101.3 2.1 %direction.5 = (f32[24,256]{1,0:T(8,128)S(1)}, f32[32,1,128]{2,1,0:T(1,128)S(1)}) custom-call(bf16[2,64,128,128]{3,2,1,0:T(8,128)(2,1)S(1)} %copy-done.3, bf16[2,64,32,128]{3,2,1,0:T(8,128)(2,1)S(1)} %copy-done.5, s32[4]{0:T(128)S(1)} %get-tuple-element.68.refs_2_, bf16[2,5,1024,128]{3,2,1,0:T(8,128)(2,1)S(1)} %get-tuple-element.69.refs_3_, ...), custom_call_target="tpu_custom_call" | custom-call | tf_op jit(solution)/shard_map/direction/pallas_call | solution.py:443
  103.4 12.1 %all_to_all.57.parts_ref = f32[32,1,128]{2,1,0:T(1,128)S(1)} all-to-all(f32[32,1,128]{2,1,0:T(1,128)S(1)} %get-tuple-element.74), channel_id=1, replica_groups=mesh['users_0'=4,'users_1'=4,'users_2'=2,'camps'=16] {'users_0','users_1..., dimensions={0} | all-to-all | bytes 32768 | tf_op jit(solution)/shard_map/all_to_all | solution.py:321
  115.5 13.8 %all_to_all.58.refs_9_ = f32[16,1,128]{2,1,0:T(1,128)S(1)} all-to-all(f32[16,1,128]{2,1,0:T(1,128)S(1)} %fold.5), channel_id=1, replica_groups=mesh['users_0'=4,'users_1'=4,'users_2'=2,'camps'=16] {'camps'}, dimensions={0} | all-to-all | bytes 16384 | tf_op jit(solution)/shard_map/all_to_all | solution.py:321
  129.3 2.1 %direction.6 = (f32[24,256]{1,0:T(8,128)S(1)}, f32[32,1,128]{2,1,0:T(1,128)S(1)}, f32[24,256]{1,0:T(8,128)S(1)}) custom-call(bf16[2,64,128,128]{3,2,1,0:T(8,128)(2,1)S(1)} %copy-done.3, bf16[2,64,32,128]{3,2,1,0:T(8,128)(2,1)S(1)} %copy-done.5, s32[4]{0:T(128)S(1)} %get-tuple-element.68.refs_2_, bf16[2,5,1024,128]{3,2,1,0:T(8,128)(2,1)S(1)} %get-tuple-element.69.refs_3_, ...), custom_call_target="tpu_custom_call" | custom-call | tf_op jit(solution)/shard_map/direction/pallas_call | solution.py:443
  131.4 11.8 %all_to_all.59.parts_ref = f32[32,1,128]{2,1,0:T(1,128)S(1)} all-to-all(f32[32,1,128]{2,1,0:T(1,128)S(1)} %get-tuple-element.77), channel_id=1, replica_groups=mesh['users_0'=4,'users_1'=4,'users_2'=2,'camps'=16] {'users_0','users_1..., dimensions={0} | all-to-all | bytes 32768 | tf_op jit(solution)/shard_map/all_to_all | solution.py:321
  143.3 13.8 %all_to_all.60.refs_8_ = f32[16,1,128]{2,1,0:T(1,128)S(1)} all-to-all(f32[16,1,128]{2,1,0:T(1,128)S(1)} %fold.6), channel_id=1, replica_groups=mesh['users_0'=4,'users_1'=4,'users_2'=2,'camps'=16] {'camps'}, dimensions={0} | all-to-all | bytes 16384 | tf_op jit(solution)/shard_map/all_to_all | solution.py:321
  157.1 2.1 %direction.7 = (f32[24,256]{1,0:T(8,128)S(1)}, f32[32,1,128]{2,1,0:T(1,128)S(1)}) custom-call(bf16[2,64,128,128]{3,2,1,0:T(8,128)(2,1)S(1)} %copy-done.3, bf16[2,64,32,128]{3,2,1,0:T(8,128)(2,1)S(1)} %copy-done.5, s32[4]{0:T(128)S(1)} %get-tuple-element.68.refs_2_, bf16[2,5,1024,128]{3,2,1,0:T(8,128)(2,1)S(1)} %get-tuple-element.69.refs_3_, ...), custom_call_target="tpu_custom_call" | custom-call | tf_op jit(solution)/shard_map/direction/pallas_call | solution.py:443
  159.2 11.8 %all_to_all.61.parts_ref = f32[32,1,128]{2,1,0:T(1,128)S(1)} all-to-all(f32[32,1,128]{2,1,0:T(1,128)S(1)} %get-tuple-element.79), channel_id=1, replica_groups=mesh['users_0'=4,'users_1'=4,'users_2'=2,'camps'=16] {'users_0','users_1..., dimensions={0} | all-to-all | bytes 32768 | tf_op jit(solution)/shard_map/all_to_all | solution.py:321
  171.1 13.8 %all_to_all.62.sums_ref = f32[16,1,128]{2,1,0:T(1,128)S(1)} all-to-all(f32[16,1,128]{2,1,0:T(1,128)S(1)} %fold.7), channel_id=1, replica_groups=mesh['users_0'=4,'users_1'=4,'users_2'=2,'camps'=16] {'camps'}, dimensions={0} | all-to-all | bytes 16384 | tf_op jit(solution)/shard_map/all_to_all | solution.py:321
  184.9 0.7 final.1
  (8 shorter events, 0.2 us)
Async XLA Ops:
  1.4 60.1 %copy-start.4 = (bf16[2,1,12,128,128]{4,3,2,1,0:T(8,128)(2,1)S(1)}, bf16[2,1,12,128,128]{4,3,2,1,0:T(8,128)(2,1)}, u32[]{:S(2)}) copy-start(bf16[2,1,12,128,128]{4,3,2,1,0:T(8,128)(2,1)} %scores_hbm.1) | copy-start | bytes 2359300
  1.4 60.1 %copy-start.6 = (bf16[24,256]{1,0:T(8,128)(2,1)S(1)}, bf16[24,256]{1,0:T(8,128)(2,1)}, u32[]{:S(2)}) copy-start(bf16[24,256]{1,0:T(8,128)(2,1)} %act_hbm.1) | copy-start | bytes 36868
  1.4 60.1 %copy-start.7 = (s32[2,1,12]{2,1,0:T(1,128)S(1)}, s32[2,1,12]{2,1,0:T(1,128)}, u32[]{:S(2)}) copy-start(s32[2,1,12]{2,1,0:T(1,128)} %param.9) | copy-start | bytes 292
  1.4 60.1 %copy-start.8 = (s32[2,1]{0,1:T(1,128)S(1)}, s32[2,1]{0,1:T(1,128)}, u32[]{:S(2)}) copy-start(s32[2,1]{0,1:T(1,128)} %param.10) | copy-start | bytes 28
  3.9 29.3 %all-to-all-start.1 = ((bf16[32,152,128]{2,1,0:T(8,128)(2,1)}), bf16[32,152,128]{2,1,0:T(8,128)(2,1)S(1)}, u32[]{:S(2)}, u32[]{:S(2)}) async-start(bf16[32,152,128]{2,1,0:T(8,128)(2,1)} %cut.1), calls=%async_computation.1 | async-start | bytes 2490368 | tf_op jit(solution)/shard_map/all_to_all | solution.py:321
  61.5 0.7 copy-start.1
  61.5 0.7 copy-start.2
  62.2 39.1 %copy-start.3 = (bf16[2,64,128,128]{3,2,1,0:T(8,128)(2,1)S(1)}, bf16[2,64,128,128]{3,2,1,0:T(8,128)(2,1)}, u32[]{:S(2)}) copy-start(bf16[2,64,128,128]{3,2,1,0:T(8,128)(2,1)} %get-tuple-element.64.refs_0_) | copy-start | bytes 12582916
  62.2 39.1 %copy-start.5 = (bf16[2,64,32,128]{3,2,1,0:T(8,128)(2,1)S(1)}, bf16[2,64,32,128]{3,2,1,0:T(8,128)(2,1)}, u32[]{:S(2)}) copy-start(bf16[2,64,32,128]{3,2,1,0:T(8,128)(2,1)} %get-tuple-element.65.refs_1_) | copy-start | bytes 3145732

commit v4 on v0

v4 whole, which is shorter than its diff:
```python
import functools

import jax
import jax.numpy as jnp
from jax import lax
from jax.experimental import pallas as pl
from jax.experimental.pallas import tpu as pltpu
from jax.sharding import Mesh
from jax.sharding import PartitionSpec as P

STEPS = 2
USERS = ("users_0", "users_1", "users_2")
USERS_CAMPS = ("users_0", "users_1", "users_2", "camps")
TILE = 128
LINES = 8
ACT = 32
UNROLL = 4
SUM_LANE = 64

VMEM = pl.BlockSpec(memory_space=pltpu.VMEM)
HBM = pl.BlockSpec(memory_space=pltpu.HBM)
PARAMS = pltpu.CompilerParams(vmem_limit_bytes=8 * 2**20)
NT = (((1,), (1,)), ((), ()))


def rounded(value):
    return value.astype(jnp.bfloat16).astype(jnp.float32)


def cut_kernel(ids_ref, prices_ref, limit_ref, scores_hbm, act_hbm, out_ref, scores, act, sems):
    load_act = pltpu.make_async_copy(act_hbm, act, sems.at[0])
    load_scores = pltpu.make_async_copy(scores_hbm, scores, sems.at[1])
    load_act.start()
    load_scores.start()
    devices = out_ref.shape[0]
    hours, campaigns = prices_ref.shape
    blocks, slots = scores.shape[0], scores.shape[2]
    owned = campaigns // TILE
    w = TILE // devices
    span = owned * w
    acts = blocks * slots * w
    values = acts + blocks * hours
    lines = values + span
    row = lax.broadcasted_iota(jnp.int32, (campaigns, campaigns), 0)
    col = lax.broadcasted_iota(jnp.int32, (campaigns, campaigns), 1)
    source = lax.rem(row, span) // w * TILE + row // span * w + lax.rem(row, w)
    pick = jnp.where(col == source, 1.0, 0.0)
    pick_half = (pick * 0.5).astype(jnp.bfloat16)
    pick = pick.astype(jnp.bfloat16)

    price, limit = prices_ref[...], limit_ref[...]
    high = rounded(price)
    middle = rounded(price - high)
    limit_high = rounded(limit)
    terms = [high, middle, price - high - middle, limit_high, limit - limit_high]
    terms.append(jnp.zeros((TILE - len(terms) * hours, campaigns), jnp.float32))
    terms = jnp.concatenate(terms, axis=0).astype(jnp.bfloat16)
    terms = lax.dot_general(pick, terms, NT, preferred_element_type=jnp.float32).astype(jnp.bfloat16)
    ids = ids_ref[...]
    for m in range(devices):
        out_ref[m, values : values + span, :] = terms[m * span : (m + 1) * span]
        out_ref[m, lines : lines + LINES, :] = ids
    load_act.wait()
    for b in range(blocks):
        own = act[:, b * TILE : (b + 1) * TILE]
        for m in range(devices):
            out_ref[m, acts + b * hours : acts + (b + 1) * hours, :] = own
    load_scores.wait()
    for b in range(blocks):
        for k in range(0, slots, owned):
            tiles = jnp.concatenate([scores[b, 0, k + j] for j in range(owned)], axis=1)
            cut = lax.dot_general(pick_half, tiles, NT, preferred_element_type=jnp.float32).astype(jnp.bfloat16)
            at = (b * slots + k) * w
            for m in range(devices):
                out_ref[m, at : at + span, :] = cut[m * span : (m + 1) * span]


def unpack(hours, blocks, rows, packets_ref, anchor_ref, limit_ref, hot_ref, acts_ref):
    devices = packets_ref.shape[0]
    campaigns = anchor_ref.shape[1]
    span = campaigns // devices
    w = TILE // devices
    act_row = blocks * rows
    values = act_row + blocks * hours
    lines = values + span
    terms = packets_ref[:, values : values + span, :].reshape(campaigns, TILE).astype(jnp.float32).T
    terms = [terms[n * hours : (n + 1) * hours] for n in range(5)]
    anchor_ref[...] = terms[0] + terms[1] + terms[2]
    limit_ref[...] = terms[3] + terms[4]
    hour = lax.broadcasted_iota(jnp.int32, (ACT - hours, TILE), 0)
    tail = jnp.where(hour == 0, 1.0, 0.0).astype(jnp.bfloat16)
    slot = lax.broadcasted_iota(jnp.int32, (rows, TILE), 0) // w
    own_slot = slot == lax.broadcasted_iota(jnp.int32, (rows, TILE), 1)
    column = lax.rem(lax.broadcasted_iota(jnp.int32, (rows, campaigns), 0), w)
    wanted = (lax.broadcasted_iota(jnp.int32, (rows, campaigns), 1) - column).astype(jnp.float32)
    ones = jnp.ones((TILE, campaigns), jnp.bfloat16)

    @pl.loop(0, devices // UNROLL)
    def _(step):
        for n in range(UNROLL):
            i = step * UNROLL + n
            ids = packets_ref[i, lines : lines + LINES, :].astype(jnp.float32)
            for b in range(blocks):
                spread = jnp.where(own_slot, ids[b : b + 1, :], 0.0).astype(jnp.bfloat16)
                first = jnp.dot(spread, ones, preferred_element_type=jnp.float32)
                hot_ref[i, b * rows : (b + 1) * rows, :] = jnp.where(first == wanted, 1.0, 0.0).astype(jnp.bfloat16)
                acts_ref[i, b * ACT : b * ACT + hours, :] = packets_ref[i, act_row + b * hours : act_row + (b + 1) * hours, :]
                acts_ref[i, b * ACT + hours : (b + 1) * ACT, :] = tail


def usage_at(lam, blocks, rows, packets_ref, hot_ref, acts_ref):
    hours, campaigns = lam.shape
    devices = packets_ref.shape[0]
    hour = lax.broadcasted_iota(jnp.int32, (ACT - hours, campaigns), 0)
    half = jnp.where(hour == 0, 0.5, 0.0)
    table = jnp.concatenate([rounded(lam) * -0.5, half], axis=0).astype(jnp.bfloat16)

    def senders(step, total):
        for n in range(UNROLL):
            i = step * UNROLL + n
            named = lax.dot_general(
                hot_ref[i], table, NT, preferred_element_type=jnp.float32
            ).astype(jnp.bfloat16)
            for b in range(blocks):
                act = acts_ref[i, b * ACT : (b + 1) * ACT, :]
                part = jnp.dot(named[b * rows : (b + 1) * rows], act, preferred_element_type=jnp.float32)
                score = packets_ref[i, b * rows : (b + 1) * rows, :].astype(jnp.float32)
                share = jnp.clip(score + part, 0.0, 1.0).astype(jnp.bfloat16)
                used = lax.dot_general(act, share, NT, preferred_element_type=jnp.float32)
                high = rounded(used)
                both = jnp.concatenate([high, used - high], axis=0).astype(jnp.bfloat16)
                hot = hot_ref[i, b * rows : (b + 1) * rows, :]
                total = total + jnp.dot(both, hot, preferred_element_type=jnp.float32)
        return total

    total = lax.fori_loop(0, devices // UNROLL, senders, jnp.zeros((2 * ACT, campaigns), jnp.float32))
    return total[:hours] + total[ACT : ACT + hours]


def scale_of(parts_ref, entries):
    squares = jnp.sum(jnp.sum(parts_ref[:, 0, :], axis=0, keepdims=True), axis=1, keepdims=True)
    return lax.rsqrt(squares / entries + 1e-06)


def moved(lam, gap, scale):
    return jnp.maximum(lam + 0.3 * (gap * scale), 0.0)


def direction_kernel(blocks, rows, entries, kind, *refs):
    if kind == "first":
        packets_ref, gap_ref, send_ref, anchor_ref, limit_ref, hot_ref, acts_ref = refs
        hours = gap_ref.shape[0]
        unpack(hours, blocks, rows, packets_ref, anchor_ref, limit_ref, hot_ref, acts_ref)
        at = anchor_ref[...]
    elif kind == "middle":
        packets_ref, anchor_ref, limit_ref, hot_ref, acts_ref, before_ref, sums_ref, gap_ref, send_ref = refs
        at = moved(anchor_ref[...], before_ref[...], scale_of(sums_ref, entries))
    elif kind == "last":
        packets_ref, anchor_ref, limit_ref, hot_ref, acts_ref, lam_ref, before_ref, sums_ref, send_ref = refs
        at = moved(lam_ref[...], before_ref[...], scale_of(sums_ref, entries))
    else:
        packets_ref, anchor_ref, limit_ref, hot_ref, acts_ref = refs[:5]
        lam_ref, before_ref, sums_ref, gap_ref, send_ref, lam_out_ref = refs[5:]
        extra = moved(lam_ref[...], before_ref[...], scale_of(sums_ref, entries))
        weight = 1.0 / (kind + 2.0)
        at = weight * anchor_ref[...] + (1.0 - weight) * extra
        lam_out_ref[...] = at
    gap = usage_at(at, blocks, rows, packets_ref, hot_ref, acts_ref) - limit_ref[...]
    line = jnp.sum(gap * gap, axis=0, keepdims=True)
    if kind != "last":
        gap_ref[...] = gap
        line = sum(line[:, n : n + TILE] for n in range(0, line.shape[1], TILE))
        send_ref[...] = jnp.broadcast_to(line[None], send_ref.shape)
        return
    hours, campaigns = gap.shape
    devices, span = send_ref.shape[:2]
    squares = jnp.broadcast_to(jnp.sum(line, axis=1, keepdims=True), (LINES, campaigns))
    results = [gap, lam_ref[...]]
    results.append(jnp.zeros((SUM_LANE - 2 * hours, campaigns), jnp.float32))
    results.append(squares)
    results.append(jnp.zeros((TILE - SUM_LANE - LINES, campaigns), jnp.float32))
    results = jnp.concatenate(results, axis=0).T
    for i in range(devices):
        send_ref[i] = results[i * span : (i + 1) * span]


def fold_kernel(last, parts_ref, out_ref):
    line = jnp.sum(parts_ref[:, 0, :], axis=0, keepdims=True)
    if last:
        lane = lax.broadcasted_iota(jnp.int32, line.shape, 1)
        line = jnp.where(lane == SUM_LANE, line, 0.0)
    out_ref[...] = jnp.broadcast_to(line[None], out_ref.shape)


def final_kernel(entries, step, anchor_ref, parts_ref, sums_ref, new_ref, dir_ref, rows):
    devices, span = parts_ref.shape[:2]
    hours, campaigns = anchor_ref.shape
    w = TILE // devices
    for m in range(devices):
        for j in range(span // w):
            rows[j * TILE + m * w : j * TILE + (m + 1) * w, :] = parts_ref[m, j * w : (j + 1) * w, :]
    results = rows[...].T
    gap, lam = results[:hours], results[hours : 2 * hours]
    scale = scale_of(sums_ref, entries)
    dir_ref[...] = gap * scale
    weight = 1.0 / (step + 2.0)
    new_ref[...] = weight * anchor_ref[...] + (1.0 - weight) * moved(lam, gap, scale)


def swapped(parts, axis):
    return lax.all_to_all(parts, axis, split_axis=0, concat_axis=0, tiled=True)


def kernel_call(body, name, out_shape, in_specs, out_specs, scratch_shapes=()):
    return pl.pallas_call(
        body,
        out_shape=out_shape,
        in_specs=in_specs,
        out_specs=out_specs,
        scratch_shapes=scratch_shapes,
        compiler_params=PARAMS,
        name=name,
    )


def on_device(scores, elig_ids, elig_counts, activity, prices, spend_limit):
    devices = lax.axis_size(USERS)
    groups = lax.axis_size("camps")
    entries = float(prices.size * devices * groups)
    hours, campaigns = prices.shape
    blocks, slots = scores.shape[0], scores.shape[2]
    w = TILE // devices
    span = campaigns // TILE * w
    rows = slots * w
    bf16, f32, i32 = jnp.bfloat16, jnp.float32, jnp.int32
    shape = jax.ShapeDtypeStruct

    slot_ids = jnp.arange(slots, dtype=i32)
    ids = jnp.where(slot_ids[None, :] < elig_counts, elig_ids[:, 0] * w, -TILE).astype(bf16)
    ids = jnp.pad(ids, ((0, LINES - blocks), (0, TILE - slots)))
    packets = kernel_call(
        cut_kernel,
        "cut",
        shape((devices, blocks * (rows + hours) + span + LINES, TILE), bf16),
        [VMEM, VMEM, VMEM, HBM, HBM],
        VMEM,
        [
            pltpu.VMEM(scores.shape, bf16),
            pltpu.VMEM(activity.shape, bf16),
            pltpu.SemaphoreType.DMA((2,)),
        ],
    )(ids, prices, spend_limit, scores, activity)
    packets = swapped(packets, USERS)

    value = shape(prices.shape, f32)
    part = shape((devices, 1, TILE), f32)

    def total_of(parts, last=False):
        folded = kernel_call(
            functools.partial(fold_kernel, last), "fold", shape((groups, 1, TILE), f32), [VMEM], VMEM
        )(parts)
        return swapped(folded, "camps")

    def direction(kind, outs, *args):
        return kernel_call(
            functools.partial(direction_kernel, blocks, rows, entries, kind),
            "direction",
            outs,
            [VMEM] * len(args),
            [VMEM] * len(outs),
        )(*args)

    kept_shapes = [
        value,
        value,
        shape((devices, blocks * rows, campaigns), bf16),
        shape((devices, blocks * ACT, TILE), bf16),
    ]
    gap, parts, *kept = direction("first", [value, part] + kept_shapes, packets)
    lam = kept[0]
    for step in range(STEPS - 1):
        sums = total_of(swapped(parts, USERS))
        gap, parts = direction("middle", [value, part], packets, *kept, gap, sums)
        sums = total_of(swapped(parts, USERS))
        gap, parts, lam = direction(step, [value, part, value], packets, *kept, lam, gap, sums)
    sums = total_of(swapped(parts, USERS))
    (parts,) = direction("last", [shape((devices, span, TILE), f32)], packets, *kept, lam, gap, sums)
    parts = swapped(parts, USERS)
    new, last = kernel_call(
        functools.partial(final_kernel, entries, STEPS - 1),
        "final",
        [value, value],
        [VMEM] * 3,
        [VMEM] * 2,
        [pltpu.VMEM((campaigns, TILE), f32)],
    )(prices, parts, total_of(parts, last=True))
    return (new, last)


def solution(mesh):
    torus = Mesh(
        mesh.devices.reshape(4, 4, 2, mesh.shape["camps"]),
        ("users_0", "users_1", "users_2", "camps"),
    )
    in_specs = (
        P(USERS, "camps", None, None, None),
        P(USERS, "camps", None),
        P(USERS, "camps"),
        P(None, USERS),
        P(None, USERS_CAMPS),
        P(None, USERS_CAMPS),
    )
    out_specs = (P(None, USERS_CAMPS), P(None, USERS_CAMPS))
    return jax.shard_map(
        on_device, mesh=torus, in_specs=in_specs, out_specs=out_specs, check_vma=False
    )
```

time: 383 us -> 212 us (0.55); the launches traced: 375 us -> 211 us
  blocking collectives: 250 us -> 143 us
  Pallas kernels: 0 us -> 62.6 us
  starting transfers between devices: 43.2 us -> 0 us
  waiting for transfers between devices: 40.2 us -> 0 us
  local copies, waits for them, and re-layouts: 19 us -> 3.32 us
  matrix products: 9.17 us -> 0 us
  other arithmetic: 9.48 us -> 1.41 us
    psum x16 -> x0, blocking collectives: 179 us -> none  [over_axes(): return functools.reduce(lax.psum, axes, value)]
    all_to_all x4 -> x9, blocking collectives: 71 us -> 143 us  [swapped(): return lax.all_to_all(parts, axis, split_axis=0, concat_axis=0, tiled=True)]
    pallas_call x0 -> x10, Pallas kernels: none -> 62.6 us  [the longest x4 60.8 us: direction(): kernel_call(functools.partial(direction_kernel, blocks, rows, entries, ki...]
    all_to_all x4 -> x0, starting transfers between devices: 43.2 us -> none  [sent_to_all(): return lax.all_to_all(copies, axis, split_axis=0, concat_axis=0, tiled=True)]
    all_to_all x4 -> x0, waiting for transfers between devices: 40.2 us -> none  [sent_to_all(): return lax.all_to_all(copies, axis, split_axis=0, concat_axis=0, tiled=True)]
    dot_general x16 -> x0, matrix products: 9.17 us -> none  [the longest x8 5.38 us: one_block(): jnp.einsum('hu,kut->hkt', act_b, share, preferred_element_type=jnp.float32)]
    and x8 -> x0, other arithmetic: 5.25 us -> none  [one_block(): picked = jnp.take(table, ids_b, axis=1)]
    dynamic_slice x8 -> x0, local copies, waits for them, and re-layouts: 4.69 us -> none  [local_usage(): lax.scan(one_block, init, (acts.transpose(1, 0, 2), tiles, id_rows, count...]
  transfers between devices with their start and end apart: 4 -> 0, of which waited for: 4 -> 0; matrix products, arithmetic and copies ran while one was open for 0% -> 0% of each run, Pallas kernels for 0% -> 0%
where the time goes in v4:
time: 212 us; the launch traced here: 211 us
  blocking collectives  143 us (67%)
  Pallas kernels  62.6 us (30%)
  local copies, waits for them, and re-layouts  3.32 us (2%)
    all_to_all x9, blocking collectives, swapped(): return lax.all_to_all(parts, axis, split_axis=0, concat_axis=0, tiled=True)  143 us
    pallas_call x4, Pallas kernels, direction(): kernel_call(functools.partial(direction_kernel, blocks, rows, entries, ki...  60.8 us

profile of v4, /device:TPU:1, one launch (start us, length us, event | category | flops | bytes accessed | tf_op | source)
XLA Modules:
  0.0 211.0 jit_solution(884382822633800795)
XLA Ops:
  0.6 0.7 broadcast_multiply_fusion
  1.3 0.7 fusion
  2.0 0.0 copy-start
  2.0 1.1 copy-done
  3.2 0.0 copy-start.1
  3.2 0.7 copy-done.1
  3.9 0.0 copy-start.3
  3.9 0.7 copy-done.3
  4.7 0.0 copy-start.4
  4.7 0.7 copy-done.4
  5.4 0.9 cut.1
  6.3 29.7 %all_to_all.45.refs_0_ = bf16[32,160,128]{2,1,0:T(8,128)(2,1)S(1)} all-to-all(bf16[32,160,128]{2,1,0:T(8,128)(2,1)S(1)} %cut.1), channel_id=1, replica_groups=mesh['users_0'=4,'users_1'=4,'users_2'=2,'camps'=16] {'users_0','users_1..., dimensions={0} | all-to-all | bytes 2621440 | tf_op jit(solution)/shard_map/all_to_all | solution.py:211
  36.0 16.4 %direction.4 = (f32[24,256]{1,0:T(8,128)S(1)}, f32[32,1,128]{2,1,0:T(1,128)S(1)}, f32[24,256]{1,0:T(8,128)S(1)}, f32[24,256]{1,0:T(8,128)S(1)}, bf16[32,96,256]{...) custom-call(bf16[32,160,128]{2,1,0:T(8,128)(2,1)S(1)} %all_to_all.45.refs_0_), custom_call_target="tpu_custom_call" | custom-call | tf_op jit(solution)/shard_map/direction/pallas_call | solution.py:265
  52.4 10.5 %all_to_all.46.parts_ref = f32[32,1,128]{2,1,0:T(1,128)S(1)} all-to-all(f32[32,1,128]{2,1,0:T(1,128)S(1)} %get-tuple-element.18), channel_id=1, replica_groups=mesh['users_0'=4,'users_1'=4,'users_2'=2,'camps'=16] {'users_0','users_1..., dimensions={0} | all-to-all | bytes 32768 | tf_op jit(solution)/shard_map/all_to_all | solution.py:211
  63.0 24.8 %all_to_all.47.refs_6_ = f32[16,1,128]{2,1,0:T(1,128)S(1)} all-to-all(f32[16,1,128]{2,1,0:T(1,128)S(1)} %fold.4), channel_id=1, replica_groups=mesh['users_0'=4,'users_1'=4,'users_2'=2,'camps'=16] {'camps'}, dimensions={0} | all-to-all | bytes 16384 | tf_op jit(solution)/shard_map/all_to_all | solution.py:211
  87.8 14.7 %direction.5 = (f32[24,256]{1,0:T(8,128)S(1)}, f32[32,1,128]{2,1,0:T(1,128)S(1)}) custom-call(bf16[32,160,128]{2,1,0:T(8,128)(2,1)S(1)} %all_to_all.45.refs_0_, f32[24,256]{1,0:T(8,128)S(1)} %get-tuple-element.13.refs_1_.refs_5_, f32[24,256]{1,0:T(8,128)S(1)} %get-tuple-element.14.refs_2_, bf16[32,96,256]{2,1,0:T(8,128)(2,1)S(1)} %get-tuple-element.15.refs_3_, ...), custom_call_target="tpu_custom_call" | custom-call | tf_op jit(solution)/shard_map/direction/pallas_call | solution.py:265
  102.6 12.1 %all_to_all.48.parts_ref = f32[32,1,128]{2,1,0:T(1,128)S(1)} all-to-all(f32[32,1,128]{2,1,0:T(1,128)S(1)} %get-tuple-element.20), channel_id=1, replica_groups=mesh['users_0'=4,'users_1'=4,'users_2'=2,'camps'=16] {'users_0','users_1..., dimensions={0} | all-to-all | bytes 32768 | tf_op jit(solution)/shard_map/all_to_all | solution.py:211
  114.7 13.8 %all_to_all.49.refs_7_ = f32[16,1,128]{2,1,0:T(1,128)S(1)} all-to-all(f32[16,1,128]{2,1,0:T(1,128)S(1)} %fold.5), channel_id=1, replica_groups=mesh['users_0'=4,'users_1'=4,'users_2'=2,'camps'=16] {'camps'}, dimensions={0} | all-to-all | bytes 16384 | tf_op jit(solution)/shard_map/all_to_all | solution.py:211
  128.6 14.7 %direction.6 = (f32[24,256]{1,0:T(8,128)S(1)}, f32[32,1,128]{2,1,0:T(1,128)S(1)}, f32[24,256]{1,0:T(8,128)S(1)}) custom-call(bf16[32,160,128]{2,1,0:T(8,128)(2,1)S(1)} %all_to_all.45.refs_0_, f32[24,256]{1,0:T(8,128)S(1)} %get-tuple-element.13.refs_1_.refs_5_, f32[24,256]{1,0:T(8,128)S(1)} %get-tuple-element.14.refs_2_, ...), custom_call_target="tpu_custom_call" | custom-call | tf_op jit(solution)/shard_map/direction/pallas_call | solution.py:265
  143.3 11.8 %all_to_all.50.parts_ref = f32[32,1,128]{2,1,0:T(1,128)S(1)} all-to-all(f32[32,1,128]{2,1,0:T(1,128)S(1)} %get-tuple-element.23), channel_id=1, replica_groups=mesh['users_0'=4,'users_1'=4,'users_2'=2,'camps'=16] {'users_0','users_1..., dimensions={0} | all-to-all | bytes 32768 | tf_op jit(solution)/shard_map/all_to_all | solution.py:211
  155.2 13.8 %all_to_all.51.refs_7_ = f32[16,1,128]{2,1,0:T(1,128)S(1)} all-to-all(f32[16,1,128]{2,1,0:T(1,128)S(1)} %fold.6), channel_id=1, replica_groups=mesh['users_0'=4,'users_1'=4,'users_2'=2,'camps'=16] {'camps'}, dimensions={0} | all-to-all | bytes 16384 | tf_op jit(solution)/shard_map/all_to_all | solution.py:211
  169.0 0.0 copy-start.2
  169.0 14.9 %direction.7 = f32[32,8,128]{2,1,0:T(8,128)S(1)} custom-call(bf16[32,160,128]{2,1,0:T(8,128)(2,1)S(1)} %all_to_all.45.refs_0_, f32[24,256]{1,0:T(8,128)S(1)} %get-tuple-element.13.refs_1_.refs_5_, f32[24,256]{1,0:T(8,128)S(1)} %get-tuple-element.14.refs_2_, bf16[32,96,256]{2,1,0:T(8,128)(2,1)S(1)} %get-tuple-element.15.refs_3_, ...), custom_call_target="tpu_custom_call" | custom-call | tf_op jit(solution)/shard_map/direction/pallas_call | solution.py:265
  183.9 12.5 %all_to_all.52.parts_ref = f32[32,8,128]{2,1,0:T(8,128)S(1)} all-to-all(f32[32,8,128]{2,1,0:T(8,128)S(1)} %direction.7), channel_id=1, replica_groups=mesh['users_0'=4,'users_1'=4,'users_2'=2,'camps'=16] {'users_0','users_1..., dimensions={0} | all-to-all | bytes 262144 | tf_op jit(solution)/shard_map/all_to_all | solution.py:211
  196.4 13.8 %all_to_all.53.sums_ref = f32[16,1,128]{2,1,0:T(1,128)S(1)} all-to-all(f32[16,1,128]{2,1,0:T(1,128)S(1)} %fold.7), channel_id=1, replica_groups=mesh['users_0'=4,'users_1'=4,'users_2'=2,'camps'=16] {'camps'}, dimensions={0} | all-to-all | bytes 16384 | tf_op jit(solution)/shard_map/all_to_all | solution.py:211
  210.3 0.0 copy-done.2
  210.3 0.7 final.1
  (5 shorter events, 0.1 us)
Async XLA Ops:
  2.0 1.1 copy-start
  3.2 0.7 copy-start.1
  3.9 0.7 copy-start.3
  4.7 0.7 copy-start.4
  169.0 41.2 %copy-start.2 = (f32[24,256]{1,0:T(8,128)S(1)}, f32[24,256]{1,0:T(8,128)}, u32[]{:S(2)}) copy-start(f32[24,256]{1,0:T(8,128)} %anchor_ref.1) | copy-start | bytes 73732

commit v5 on v4

--- a/solution.py
+++ b/solution.py
@@ -14,7 +14,8 @@
 TILE = 128
 LINES = 8
 ACT = 32
-UNROLL = 4
+CHUNK = 16
+UNROLL = 8
 SUM_LANE = 64
 
 VMEM = pl.BlockSpec(memory_space=pltpu.VMEM)
@@ -89,10 +90,13 @@
     limit_ref[...] = terms[3] + terms[4]
     hour = lax.broadcasted_iota(jnp.int32, (ACT - hours, TILE), 0)
     tail = jnp.where(hour == 0, 1.0, 0.0).astype(jnp.bfloat16)
-    slot = lax.broadcasted_iota(jnp.int32, (rows, TILE), 0) // w
-    own_slot = slot == lax.broadcasted_iota(jnp.int32, (rows, TILE), 1)
-    column = lax.rem(lax.broadcasted_iota(jnp.int32, (rows, campaigns), 0), w)
-    wanted = (lax.broadcasted_iota(jnp.int32, (rows, campaigns), 1) - column).astype(jnp.float32)
+    padded = hot_ref.shape[1]
+    row = lax.broadcasted_iota(jnp.int32, (padded, TILE), 0)
+    own_slot = lax.rem(row, rows) // w == lax.broadcasted_iota(jnp.int32, (padded, TILE), 1)
+    row_block = row // rows
+    row = lax.broadcasted_iota(jnp.int32, (padded, campaigns), 0)
+    wanted = lax.broadcasted_iota(jnp.int32, (padded, campaigns), 1) - lax.rem(row, w)
+    wanted = jnp.where(row < blocks * rows, wanted, -2 * TILE).astype(jnp.float32)
     ones = jnp.ones((TILE, campaigns), jnp.bfloat16)
 
     @pl.loop(0, devices // UNROLL)
@@ -100,40 +104,53 @@
         for n in range(UNROLL):
             i = step * UNROLL + n
             ids = packets_ref[i, lines : lines + LINES, :].astype(jnp.float32)
+            spread = jnp.zeros((padded, TILE), jnp.float32)
             for b in range(blocks):
-                spread = jnp.where(own_slot, ids[b : b + 1, :], 0.0).astype(jnp.bfloat16)
-                first = jnp.dot(spread, ones, preferred_element_type=jnp.float32)
-                hot_ref[i, b * rows : (b + 1) * rows, :] = jnp.where(first == wanted, 1.0, 0.0).astype(jnp.bfloat16)
+                mine = jnp.logical_and(own_slot, row_block == b)
+                spread = jnp.where(mine, ids[b : b + 1, :], spread)
                 acts_ref[i, b * ACT : b * ACT + hours, :] = packets_ref[i, act_row + b * hours : act_row + (b + 1) * hours, :]
                 acts_ref[i, b * ACT + hours : (b + 1) * ACT, :] = tail
-
-
-def usage_at(lam, blocks, rows, packets_ref, hot_ref, acts_ref):
+            first = jnp.dot(spread.astype(jnp.bfloat16), ones, preferred_element_type=jnp.float32)
+            hot_ref[i] = jnp.where(first == wanted, 1.0, 0.0).astype(jnp.bfloat16)
+
+
+def usage_at(lam, blocks, rows, packets_ref, hot_ref, acts_ref, named_ref, share_ref, used_ref):
     hours, campaigns = lam.shape
-    devices = packets_ref.shape[0]
+    devices, padded = hot_ref.shape[:2]
+    chunk = share_ref.shape[0]
+    listed = blocks * rows
     hour = lax.broadcasted_iota(jnp.int32, (ACT - hours, campaigns), 0)
     half = jnp.where(hour == 0, 0.5, 0.0)
-    table = jnp.concatenate([rounded(lam) * -0.5, half], axis=0).astype(jnp.bfloat16)
+    table = jnp.concatenate([rounded(lam) * -0.5, half] * blocks, axis=0).astype(jnp.bfloat16)
+    row = lax.broadcasted_iota(jnp.int32, (padded, blocks * ACT), 0)
+    own = row // rows == lax.broadcasted_iota(jnp.int32, (padded, blocks * ACT), 1) // ACT
+    block = lax.broadcasted_iota(jnp.int32, (ACT, padded), 1) // rows
+    if listed < padded:
+        share_ref[:, listed:, :] = jnp.zeros((chunk, padded - listed, TILE), jnp.bfloat16)
 
     def senders(step, total):
-        for n in range(UNROLL):
-            i = step * UNROLL + n
-            named = lax.dot_general(
-                hot_ref[i], table, NT, preferred_element_type=jnp.float32
-            ).astype(jnp.bfloat16)
-            for b in range(blocks):
-                act = acts_ref[i, b * ACT : (b + 1) * ACT, :]
-                part = jnp.dot(named[b * rows : (b + 1) * rows], act, preferred_element_type=jnp.float32)
-                score = packets_ref[i, b * rows : (b + 1) * rows, :].astype(jnp.float32)
-                share = jnp.clip(score + part, 0.0, 1.0).astype(jnp.bfloat16)
-                used = lax.dot_general(act, share, NT, preferred_element_type=jnp.float32)
-                high = rounded(used)
-                both = jnp.concatenate([high, used - high], axis=0).astype(jnp.bfloat16)
-                hot = hot_ref[i, b * rows : (b + 1) * rows, :]
-                total = total + jnp.dot(both, hot, preferred_element_type=jnp.float32)
-        return total
-
-    total = lax.fori_loop(0, devices // UNROLL, senders, jnp.zeros((2 * ACT, campaigns), jnp.float32))
+        first = step * chunk
+        hot = [hot_ref[first + n] for n in range(chunk)]
+        for n in range(chunk):
+            named = lax.dot_general(hot[n], table, NT, preferred_element_type=jnp.float32)
+            named_ref[n] = jnp.where(own, named, 0.0).astype(jnp.bfloat16)
+        for n in range(chunk):
+            part = jnp.dot(named_ref[n, :listed, :], acts_ref[first + n], preferred_element_type=jnp.float32)
+            score = packets_ref[first + n, :listed, :].astype(jnp.float32)
+            share_ref[n, :listed, :] = jnp.clip(score + part, 0.0, 1.0).astype(jnp.bfloat16)
+        for n in range(chunk):
+            each = lax.dot_general(acts_ref[first + n], share_ref[n], NT, preferred_element_type=jnp.float32)
+            used = each[:ACT]
+            for b in range(1, blocks):
+                used = jnp.where(block == b, each[b * ACT : (b + 1) * ACT], used)
+            high = rounded(used)
+            both = jnp.concatenate([high, used - high], axis=0).astype(jnp.bfloat16)
+            used_ref[:, n * padded : (n + 1) * padded] = both
+        hot = hot_ref[pl.ds(first, chunk)].reshape(chunk * padded, campaigns)
+        return total + jnp.dot(used_ref[...], hot, preferred_element_type=jnp.float32)
+
+    total = jnp.zeros((2 * ACT, campaigns), jnp.float32)
+    total = lax.fori_loop(0, devices // chunk, senders, total)
     return total[:hours] + total[ACT : ACT + hours]
 
 
@@ -147,6 +164,7 @@
 
 
 def direction_kernel(blocks, rows, entries, kind, *refs):
+    refs, scratch = refs[:-3], refs[-3:]
     if kind == "first":
         packets_ref, gap_ref, send_ref, anchor_ref, limit_ref, hot_ref, acts_ref = refs
         hours = gap_ref.shape[0]
@@ -165,7 +183,7 @@
         weight = 1.0 / (kind + 2.0)
         at = weight * anchor_ref[...] + (1.0 - weight) * extra
         lam_out_ref[...] = at
-    gap = usage_at(at, blocks, rows, packets_ref, hot_ref, acts_ref) - limit_ref[...]
+    gap = usage_at(at, blocks, rows, packets_ref, hot_ref, acts_ref, *scratch) - limit_ref[...]
     line = jnp.sum(gap * gap, axis=0, keepdims=True)
     if kind != "last":
         gap_ref[...] = gap
@@ -232,6 +250,8 @@
     w = TILE // devices
     span = campaigns // TILE * w
     rows = slots * w
+    padded = pl.cdiv(blocks * rows, TILE) * TILE
+    chunk = min(CHUNK, devices)
     bf16, f32, i32 = jnp.bfloat16, jnp.float32, jnp.int32
     shape = jax.ShapeDtypeStruct
 
@@ -268,12 +288,17 @@
             outs,
             [VMEM] * len(args),
             [VMEM] * len(outs),
+            [
+                pltpu.VMEM((chunk, padded, blocks * ACT), bf16),
+                pltpu.VMEM((chunk, padded, TILE), bf16),
+                pltpu.VMEM((2 * ACT, chunk * padded), bf16),
+            ],
         )(*args)
 
     kept_shapes = [
         value,
         value,
-        shape((devices, blocks * rows, campaigns), bf16),
+        shape((devices, padded, campaigns), bf16),
         shape((devices, blocks * ACT, TILE), bf16),
     ]
     gap, parts, *kept = direction("first", [value, part] + kept_shapes, packets)

time: 212 us -> 163 us (0.77)
  Pallas kernels: 62.6 us -> 13.7 us
    pallas_call x4, Pallas kernels: 60.8 us -> 12 us  [direction(): kernel_call(functools.partial(direction_kernel, blocks, rows, entries, ki...]
where the time goes in v5:
time: 163 us; the launch traced here: 162 us
  blocking collectives  143 us (88%)
  Pallas kernels  13.7 us (8%)
  local copies, waits for them, and re-layouts  3.32 us (2%)
    all_to_all x9, blocking collectives, swapped(): return lax.all_to_all(parts, axis, split_axis=0, concat_axis=0, tiled=True)  143 us
    pallas_call x4, Pallas kernels, direction(): kernel_call(functools.partial(direction_kernel, blocks, rows, entries, ki...  12 us
    unnamed x10, local copies, waits for them, and re-layouts  3.32 us

profile of v5, /device:TPU:1, one launch (start us, length us, event | category | flops | bytes accessed | tf_op | source)
XLA Modules:
  0.0 162.2 jit_solution(8670252681378639599)
XLA Ops:
  0.6 0.7 broadcast_multiply_fusion
  1.3 0.7 fusion
  2.0 0.0 copy-start
  2.0 1.1 copy-done
  3.2 0.0 copy-start.1
  3.2 0.7 copy-done.1
  3.9 0.0 copy-start.3
  3.9 0.7 copy-done.3
  4.7 0.0 copy-start.4
  4.7 0.7 copy-done.4
  5.4 0.9 cut.1
  6.3 29.7 %all_to_all.45.refs_0_ = bf16[32,160,128]{2,1,0:T(8,128)(2,1)S(1)} all-to-all(bf16[32,160,128]{2,1,0:T(8,128)(2,1)S(1)} %cut.1), channel_id=1, replica_groups=mesh['users_0'=4,'users_1'=4,'users_2'=2,'camps'=16] {'users_0','users_1..., dimensions={0} | all-to-all | bytes 2621440 | tf_op jit(solution)/shard_map/all_to_all | solution.py:229
  36.0 3.8 %direction.4 = (f32[24,256]{1,0:T(8,128)S(1)}, f32[32,1,128]{2,1,0:T(1,128)S(1)}, f32[24,256]{1,0:T(8,128)S(1)}, f32[24,256]{1,0:T(8,128)S(1)}, bf16[32,128,256]...) custom-call(bf16[32,160,128]{2,1,0:T(8,128)(2,1)S(1)} %all_to_all.45.refs_0_), custom_call_target="tpu_custom_call" | custom-call | tf_op jit(solution)/shard_map/direction/pallas_call | solution.py:285
  39.8 10.5 %all_to_all.46.parts_ref = f32[32,1,128]{2,1,0:T(1,128)S(1)} all-to-all(f32[32,1,128]{2,1,0:T(1,128)S(1)} %get-tuple-element.18), channel_id=1, replica_groups=mesh['users_0'=4,'users_1'=4,'users_2'=2,'camps'=16] {'users_0','users_1..., dimensions={0} | all-to-all | bytes 32768 | tf_op jit(solution)/shard_map/all_to_all | solution.py:229
  50.4 24.8 %all_to_all.47.refs_6_ = f32[16,1,128]{2,1,0:T(1,128)S(1)} all-to-all(f32[16,1,128]{2,1,0:T(1,128)S(1)} %fold.4), channel_id=1, replica_groups=mesh['users_0'=4,'users_1'=4,'users_2'=2,'camps'=16] {'camps'}, dimensions={0} | all-to-all | bytes 16384 | tf_op jit(solution)/shard_map/all_to_all | solution.py:229
  75.2 2.7 %direction.5 = (f32[24,256]{1,0:T(8,128)S(1)}, f32[32,1,128]{2,1,0:T(1,128)S(1)}) custom-call(bf16[32,160,128]{2,1,0:T(8,128)(2,1)S(1)} %all_to_all.45.refs_0_, f32[24,256]{1,0:T(8,128)S(1)} %get-tuple-element.13.refs_1_.refs_5_, f32[24,256]{1,0:T(8,128)S(1)} %get-tuple-element.14.refs_2_, bf16[32,128,256]{2,1,0:T(8,128)(2,1)S(1)} %get-tuple-element.15.refs_3_, ...), custom_call_target="tpu_custom_call" | custom-call | tf_op jit(solution)/shard_map/direction/pallas_call | solution.py:285
  77.9 12.1 %all_to_all.48.parts_ref = f32[32,1,128]{2,1,0:T(1,128)S(1)} all-to-all(f32[32,1,128]{2,1,0:T(1,128)S(1)} %get-tuple-element.20), channel_id=1, replica_groups=mesh['users_0'=4,'users_1'=4,'users_2'=2,'camps'=16] {'users_0','users_1..., dimensions={0} | all-to-all | bytes 32768 | tf_op jit(solution)/shard_map/all_to_all | solution.py:229
  90.0 13.8 %all_to_all.49.refs_7_ = f32[16,1,128]{2,1,0:T(1,128)S(1)} all-to-all(f32[16,1,128]{2,1,0:T(1,128)S(1)} %fold.5), channel_id=1, replica_groups=mesh['users_0'=4,'users_1'=4,'users_2'=2,'camps'=16] {'camps'}, dimensions={0} | all-to-all | bytes 16384 | tf_op jit(solution)/shard_map/all_to_all | solution.py:229
  103.9 2.7 %direction.6 = (f32[24,256]{1,0:T(8,128)S(1)}, f32[32,1,128]{2,1,0:T(1,128)S(1)}, f32[24,256]{1,0:T(8,128)S(1)}) custom-call(bf16[32,160,128]{2,1,0:T(8,128)(2,1)S(1)} %all_to_all.45.refs_0_, f32[24,256]{1,0:T(8,128)S(1)} %get-tuple-element.13.refs_1_.refs_5_, f32[24,256]{1,0:T(8,128)S(1)} %get-tuple-element.14.refs_2_, ...), custom_call_target="tpu_custom_call" | custom-call | tf_op jit(solution)/shard_map/direction/pallas_call | solution.py:285
  106.5 11.8 %all_to_all.50.parts_ref = f32[32,1,128]{2,1,0:T(1,128)S(1)} all-to-all(f32[32,1,128]{2,1,0:T(1,128)S(1)} %get-tuple-element.23), channel_id=1, replica_groups=mesh['users_0'=4,'users_1'=4,'users_2'=2,'camps'=16] {'users_0','users_1..., dimensions={0} | all-to-all | bytes 32768 | tf_op jit(solution)/shard_map/all_to_all | solution.py:229
  118.4 13.8 %all_to_all.51.refs_7_ = f32[16,1,128]{2,1,0:T(1,128)S(1)} all-to-all(f32[16,1,128]{2,1,0:T(1,128)S(1)} %fold.6), channel_id=1, replica_groups=mesh['users_0'=4,'users_1'=4,'users_2'=2,'camps'=16] {'camps'}, dimensions={0} | all-to-all | bytes 16384 | tf_op jit(solution)/shard_map/all_to_all | solution.py:229
  132.2 0.0 copy-start.2
  132.3 2.8 %direction.7 = f32[32,8,128]{2,1,0:T(8,128)S(1)} custom-call(bf16[32,160,128]{2,1,0:T(8,128)(2,1)S(1)} %all_to_all.45.refs_0_, f32[24,256]{1,0:T(8,128)S(1)} %get-tuple-element.13.refs_1_.refs_5_, f32[24,256]{1,0:T(8,128)S(1)} %get-tuple-element.14.refs_2_, bf16[32,128,256]{2,1,0:T(8,128)(2,1)S(1)} %get-tuple-element.15.refs_3_, ...), custom_call_target="tpu_custom_call" | custom-call | tf_op jit(solution)/shard_map/direction/pallas_call | solution.py:285
  135.1 12.5 %all_to_all.52.parts_ref = f32[32,8,128]{2,1,0:T(8,128)S(1)} all-to-all(f32[32,8,128]{2,1,0:T(8,128)S(1)} %direction.7), channel_id=1, replica_groups=mesh['users_0'=4,'users_1'=4,'users_2'=2,'camps'=16] {'users_0','users_1..., dimensions={0} | all-to-all | bytes 262144 | tf_op jit(solution)/shard_map/all_to_all | solution.py:229
  147.6 13.8 %all_to_all.53.sums_ref = f32[16,1,128]{2,1,0:T(1,128)S(1)} all-to-all(f32[16,1,128]{2,1,0:T(1,128)S(1)} %fold.7), channel_id=1, replica_groups=mesh['users_0'=4,'users_1'=4,'users_2'=2,'camps'=16] {'camps'}, dimensions={0} | all-to-all | bytes 16384 | tf_op jit(solution)/shard_map/all_to_all | solution.py:229
  161.4 0.0 copy-done.2
  161.4 0.7 final.1
  (5 shorter events, 0.1 us)
Async XLA Ops:
  2.0 1.1 copy-start
  3.2 0.7 copy-start.1
  3.9 0.7 copy-start.3
  4.7 0.7 copy-start.4
  132.2 29.2 %copy-start.2 = (f32[24,256]{1,0:T(8,128)S(1)}, f32[24,256]{1,0:T(8,128)}, u32[]{:S(2)}) copy-start(f32[24,256]{1,0:T(8,128)} %anchor_ref.1) | copy-start | bytes 73732

commit v6 on v5

--- a/solution.py
+++ b/solution.py
@@ -14,7 +14,7 @@
 TILE = 128
 LINES = 8
 ACT = 32
-CHUNK = 16
+CHUNK = 32
 UNROLL = 8
 SUM_LANE = 64
 
@@ -28,13 +28,14 @@
     return value.astype(jnp.bfloat16).astype(jnp.float32)
 
 
-def cut_kernel(ids_ref, prices_ref, limit_ref, scores_hbm, act_hbm, out_ref, scores, act, sems):
-    load_act = pltpu.make_async_copy(act_hbm, act, sems.at[0])
-    load_scores = pltpu.make_async_copy(scores_hbm, scores, sems.at[1])
-    load_act.start()
-    load_scores.start()
+def cut_kernel(scores_hbm, ids_hbm, counts_hbm, prices_hbm, limit_hbm, act_hbm, out_ref, *scratch):
+    scores, ids, counts, prices, limits, act, sems = scratch
+    sources = (scores_hbm, ids_hbm, counts_hbm, prices_hbm, limit_hbm, act_hbm)
+    loads = [pltpu.make_async_copy(sources[n], scratch[n], sems.at[n]) for n in range(len(sources))]
+    for load in loads:
+        load.start()
     devices = out_ref.shape[0]
-    hours, campaigns = prices_ref.shape
+    hours, campaigns = prices.shape
     blocks, slots = scores.shape[0], scores.shape[2]
     owned = campaigns // TILE
     w = TILE // devices
@@ -49,7 +50,9 @@
     pick_half = (pick * 0.5).astype(jnp.bfloat16)
     pick = pick.astype(jnp.bfloat16)
 
-    price, limit = prices_ref[...], limit_ref[...]
+    loads[3].wait()
+    loads[4].wait()
+    price, limit = prices[...], limits[...]
     high = rounded(price)
     middle = rounded(price - high)
     limit_high = rounded(limit)
@@ -57,16 +60,25 @@
     terms.append(jnp.zeros((TILE - len(terms) * hours, campaigns), jnp.float32))
     terms = jnp.concatenate(terms, axis=0).astype(jnp.bfloat16)
     terms = lax.dot_general(pick, terms, NT, preferred_element_type=jnp.float32).astype(jnp.bfloat16)
-    ids = ids_ref[...]
+    loads[1].wait()
+    loads[2].wait()
+    row = lax.broadcasted_iota(jnp.int32, (LINES, TILE), 0)
+    lane = lax.broadcasted_iota(jnp.int32, (LINES, TILE), 1)
+    entries = jnp.full((LINES, TILE), -TILE, jnp.int32)
+    for b in range(blocks):
+        for k in range(slots):
+            here = jnp.logical_and(row == b, lane == k)
+            entries = jnp.where(here, jnp.where(k < counts[b], ids[b, 0, k] * w, -TILE), entries)
+    entries = entries.astype(jnp.float32).astype(jnp.bfloat16)
     for m in range(devices):
         out_ref[m, values : values + span, :] = terms[m * span : (m + 1) * span]
-        out_ref[m, lines : lines + LINES, :] = ids
-    load_act.wait()
+        out_ref[m, lines : lines + LINES, :] = entries
+    loads[5].wait()
     for b in range(blocks):
         own = act[:, b * TILE : (b + 1) * TILE]
         for m in range(devices):
             out_ref[m, acts + b * hours : acts + (b + 1) * hours, :] = own
-    load_scores.wait()
+    loads[0].wait()
     for b in range(blocks):
         for k in range(0, slots, owned):
             tiles = jnp.concatenate([scores[b, 0, k + j] for j in range(owned)], axis=1)
@@ -122,20 +134,20 @@
     hour = lax.broadcasted_iota(jnp.int32, (ACT - hours, campaigns), 0)
     half = jnp.where(hour == 0, 0.5, 0.0)
     table = jnp.concatenate([rounded(lam) * -0.5, half] * blocks, axis=0).astype(jnp.bfloat16)
-    row = lax.broadcasted_iota(jnp.int32, (padded, blocks * ACT), 0)
-    own = row // rows == lax.broadcasted_iota(jnp.int32, (padded, blocks * ACT), 1) // ACT
+    row = lax.broadcasted_iota(jnp.int32, (listed, blocks * ACT), 0)
+    own = row // rows == lax.broadcasted_iota(jnp.int32, (listed, blocks * ACT), 1) // ACT
     block = lax.broadcasted_iota(jnp.int32, (ACT, padded), 1) // rows
     if listed < padded:
         share_ref[:, listed:, :] = jnp.zeros((chunk, padded - listed, TILE), jnp.bfloat16)
 
     def senders(step, total):
         first = step * chunk
-        hot = [hot_ref[first + n] for n in range(chunk)]
+        hot = [hot_ref[first + n, :listed, :] for n in range(chunk)]
         for n in range(chunk):
             named = lax.dot_general(hot[n], table, NT, preferred_element_type=jnp.float32)
             named_ref[n] = jnp.where(own, named, 0.0).astype(jnp.bfloat16)
         for n in range(chunk):
-            part = jnp.dot(named_ref[n, :listed, :], acts_ref[first + n], preferred_element_type=jnp.float32)
+            part = jnp.dot(named_ref[n], acts_ref[first + n], preferred_element_type=jnp.float32)
             score = packets_ref[first + n, :listed, :].astype(jnp.float32)
             share_ref[n, :listed, :] = jnp.clip(score + part, 0.0, 1.0).astype(jnp.bfloat16)
         for n in range(chunk):
@@ -255,21 +267,23 @@
     bf16, f32, i32 = jnp.bfloat16, jnp.float32, jnp.int32
     shape = jax.ShapeDtypeStruct
 
-    slot_ids = jnp.arange(slots, dtype=i32)
-    ids = jnp.where(slot_ids[None, :] < elig_counts, elig_ids[:, 0] * w, -TILE).astype(bf16)
-    ids = jnp.pad(ids, ((0, LINES - blocks), (0, TILE - slots)))
+    sources = (scores, elig_ids, elig_counts[:, 0], prices, spend_limit, activity)
     packets = kernel_call(
         cut_kernel,
         "cut",
         shape((devices, blocks * (rows + hours) + span + LINES, TILE), bf16),
-        [VMEM, VMEM, VMEM, HBM, HBM],
+        [HBM] * len(sources),
         VMEM,
         [
             pltpu.VMEM(scores.shape, bf16),
+            pltpu.SMEM(elig_ids.shape, i32),
+            pltpu.SMEM((blocks,), i32),
+            pltpu.VMEM(prices.shape, f32),
+            pltpu.VMEM(prices.shape, f32),
             pltpu.VMEM(activity.shape, bf16),
-            pltpu.SemaphoreType.DMA((2,)),
+            pltpu.SemaphoreType.DMA((len(sources),)),
         ],
-    )(ids, prices, spend_limit, scores, activity)
+    )(*(pltpu.with_memory_space_constraint(source, pltpu.HBM) for source in sources))
     packets = swapped(packets, USERS)
 
     value = shape(prices.shape, f32)
@@ -289,7 +303,7 @@
             [VMEM] * len(args),
             [VMEM] * len(outs),
             [
-                pltpu.VMEM((chunk, padded, blocks * ACT), bf16),
+                pltpu.VMEM((chunk, blocks * rows, blocks * ACT), bf16),
                 pltpu.VMEM((chunk, padded, TILE), bf16),
                 pltpu.VMEM((2 * ACT, chunk * padded), bf16),
             ],

time: 163 us -> 157 us (0.963)
  local copies, waits for them, and re-layouts: 3.32 us -> 0.01 us
    unnamed x10 -> x2, local copies, waits for them, and re-layouts: 3.32 us -> 0.01 us
    pallas_call x4, Pallas kernels: 12 us -> 9.76 us  [direction(): kernel_call(functools.partial(direction_kernel, blocks, rows, entries, ki...]
where the time goes in v6:
time: 157 us; the launch traced here: 156 us
  blocking collectives  143 us (91%)
  Pallas kernels  12.6 us (8%)
    all_to_all x9, blocking collectives, swapped(): return lax.all_to_all(parts, axis, split_axis=0, concat_axis=0, tiled=True)  143 us
    pallas_call x4, Pallas kernels, direction(): kernel_call(functools.partial(direction_kernel, blocks, rows, entries, ki...  9.76 us

profile of v6, /device:TPU:1, one launch (start us, length us, event | category | flops | bytes accessed | tf_op | source)
XLA Modules:
  0.0 156.3 jit_solution(604482058828782264)
XLA Ops:
  0.6 2.0 %cut.1 = bf16[32,160,128]{2,1,0:T(8,128)(2,1)S(1)} custom-call(bf16[2,1,12,128,128]{4,3,2,1,0:T(8,128)(2,1)} %scores_hbm.1, s32[2,1,12]{2,1,0:T(1,128)} %ids_hbm.1, s32[2]{0:T(128)} %bitcast.1, f32[24,256]{1,0:T(8,128)} %anchor_ref.1, f32[24,256]{1,0:T(8,128)} %limit_hbm.1, bf16[24,256]{1,0:T(8,128)(2,1)} %act_hbm.1), custom_call_target="tpu_custom_call" | custom-call | tf_op jit(solution)/shard_map/cut/pallas_call | solution.py:271
  2.6 29.7 %all_to_all.45.refs_0_ = bf16[32,160,128]{2,1,0:T(8,128)(2,1)S(1)} all-to-all(bf16[32,160,128]{2,1,0:T(8,128)(2,1)S(1)} %cut.1), channel_id=1, replica_groups=mesh['users_0'=4,'users_1'=4,'users_2'=2,'camps'=16] {'users_0','users_1..., dimensions={0} | all-to-all | bytes 2621440 | tf_op jit(solution)/shard_map/all_to_all | solution.py:241
  32.3 3.3 %direction.4 = (f32[24,256]{1,0:T(8,128)S(1)}, f32[32,1,128]{2,1,0:T(1,128)S(1)}, f32[24,256]{1,0:T(8,128)S(1)}, f32[24,256]{1,0:T(8,128)S(1)}, bf16[32,128,256]...) custom-call(bf16[32,160,128]{2,1,0:T(8,128)(2,1)S(1)} %all_to_all.45.refs_0_), custom_call_target="tpu_custom_call" | custom-call | tf_op jit(solution)/shard_map/direction/pallas_call | solution.py:299
  35.6 10.5 %all_to_all.46.parts_ref = f32[32,1,128]{2,1,0:T(1,128)S(1)} all-to-all(f32[32,1,128]{2,1,0:T(1,128)S(1)} %get-tuple-element.18), channel_id=1, replica_groups=mesh['users_0'=4,'users_1'=4,'users_2'=2,'camps'=16] {'users_0','users_1..., dimensions={0} | all-to-all | bytes 32768 | tf_op jit(solution)/shard_map/all_to_all | solution.py:241
  46.1 24.8 %all_to_all.47.refs_6_ = f32[16,1,128]{2,1,0:T(1,128)S(1)} all-to-all(f32[16,1,128]{2,1,0:T(1,128)S(1)} %fold.4), channel_id=1, replica_groups=mesh['users_0'=4,'users_1'=4,'users_2'=2,'camps'=16] {'camps'}, dimensions={0} | all-to-all | bytes 16384 | tf_op jit(solution)/shard_map/all_to_all | solution.py:241
  71.0 2.1 %direction.5 = (f32[24,256]{1,0:T(8,128)S(1)}, f32[32,1,128]{2,1,0:T(1,128)S(1)}) custom-call(bf16[32,160,128]{2,1,0:T(8,128)(2,1)S(1)} %all_to_all.45.refs_0_, f32[24,256]{1,0:T(8,128)S(1)} %get-tuple-element.13.refs_1_.refs_5_, f32[24,256]{1,0:T(8,128)S(1)} %get-tuple-element.14.refs_2_, bf16[32,128,256]{2,1,0:T(8,128)(2,1)S(1)} %get-tuple-element.15.refs_3_, ...), custom_call_target="tpu_custom_call" | custom-call | tf_op jit(solution)/shard_map/direction/pallas_call | solution.py:299
  73.1 12.1 %all_to_all.48.parts_ref = f32[32,1,128]{2,1,0:T(1,128)S(1)} all-to-all(f32[32,1,128]{2,1,0:T(1,128)S(1)} %get-tuple-element.20), channel_id=1, replica_groups=mesh['users_0'=4,'users_1'=4,'users_2'=2,'camps'=16] {'users_0','users_1..., dimensions={0} | all-to-all | bytes 32768 | tf_op jit(solution)/shard_map/all_to_all | solution.py:241
  85.2 13.8 %all_to_all.49.refs_7_ = f32[16,1,128]{2,1,0:T(1,128)S(1)} all-to-all(f32[16,1,128]{2,1,0:T(1,128)S(1)} %fold.5), channel_id=1, replica_groups=mesh['users_0'=4,'users_1'=4,'users_2'=2,'camps'=16] {'camps'}, dimensions={0} | all-to-all | bytes 16384 | tf_op jit(solution)/shard_map/all_to_all | solution.py:241
  99.1 2.1 %direction.6 = (f32[24,256]{1,0:T(8,128)S(1)}, f32[32,1,128]{2,1,0:T(1,128)S(1)}, f32[24,256]{1,0:T(8,128)S(1)}) custom-call(bf16[32,160,128]{2,1,0:T(8,128)(2,1)S(1)} %all_to_all.45.refs_0_, f32[24,256]{1,0:T(8,128)S(1)} %get-tuple-element.13.refs_1_.refs_5_, f32[24,256]{1,0:T(8,128)S(1)} %get-tuple-element.14.refs_2_, ...), custom_call_target="tpu_custom_call" | custom-call | tf_op jit(solution)/shard_map/direction/pallas_call | solution.py:299
  101.2 11.8 %all_to_all.50.parts_ref = f32[32,1,128]{2,1,0:T(1,128)S(1)} all-to-all(f32[32,1,128]{2,1,0:T(1,128)S(1)} %get-tuple-element.23), channel_id=1, replica_groups=mesh['users_0'=4,'users_1'=4,'users_2'=2,'camps'=16] {'users_0','users_1..., dimensions={0} | all-to-all | bytes 32768 | tf_op jit(solution)/shard_map/all_to_all | solution.py:241
  113.1 13.8 %all_to_all.51.refs_7_ = f32[16,1,128]{2,1,0:T(1,128)S(1)} all-to-all(f32[16,1,128]{2,1,0:T(1,128)S(1)} %fold.6), channel_id=1, replica_groups=mesh['users_0'=4,'users_1'=4,'users_2'=2,'camps'=16] {'camps'}, dimensions={0} | all-to-all | bytes 16384 | tf_op jit(solution)/shard_map/all_to_all | solution.py:241
  126.9 0.0 copy-start
  126.9 2.3 %direction.7 = f32[32,8,128]{2,1,0:T(8,128)S(1)} custom-call(bf16[32,160,128]{2,1,0:T(8,128)(2,1)S(1)} %all_to_all.45.refs_0_, f32[24,256]{1,0:T(8,128)S(1)} %get-tuple-element.13.refs_1_.refs_5_, f32[24,256]{1,0:T(8,128)S(1)} %get-tuple-element.14.refs_2_, bf16[32,128,256]{2,1,0:T(8,128)(2,1)S(1)} %get-tuple-element.15.refs_3_, ...), custom_call_target="tpu_custom_call" | custom-call | tf_op jit(solution)/shard_map/direction/pallas_call | solution.py:299
  129.2 12.5 %all_to_all.52.parts_ref = f32[32,8,128]{2,1,0:T(8,128)S(1)} all-to-all(f32[32,8,128]{2,1,0:T(8,128)S(1)} %direction.7), channel_id=1, replica_groups=mesh['users_0'=4,'users_1'=4,'users_2'=2,'camps'=16] {'users_0','users_1..., dimensions={0} | all-to-all | bytes 262144 | tf_op jit(solution)/shard_map/all_to_all | solution.py:241
  141.7 13.8 %all_to_all.53.sums_ref = f32[16,1,128]{2,1,0:T(1,128)S(1)} all-to-all(f32[16,1,128]{2,1,0:T(1,128)S(1)} %fold.7), channel_id=1, replica_groups=mesh['users_0'=4,'users_1'=4,'users_2'=2,'camps'=16] {'camps'}, dimensions={0} | all-to-all | bytes 16384 | tf_op jit(solution)/shard_map/all_to_all | solution.py:241
  155.5 0.0 copy-done
  155.5 0.7 final.1
  (4 shorter events, 0.1 us)
Async XLA Ops:
  126.9 28.6 %copy-start = (f32[24,256]{1,0:T(8,128)S(1)}, f32[24,256]{1,0:T(8,128)}, u32[]{:S(2)}) copy-start(f32[24,256]{1,0:T(8,128)} %anchor_ref.1) | copy-start | bytes 73732

commit v7 on v6

--- a/solution.py
+++ b/solution.py
@@ -13,6 +13,7 @@
 USERS_CAMPS = ("users_0", "users_1", "users_2", "camps")
 TILE = 128
 LINES = 8
+TERMS = 5
 ACT = 32
 CHUNK = 32
 UNROLL = 8
@@ -22,6 +23,11 @@
 HBM = pl.BlockSpec(memory_space=pltpu.HBM)
 PARAMS = pltpu.CompilerParams(vmem_limit_bytes=8 * 2**20)
 NT = (((1,), (1,)), ((), ()))
+
+
+def entry_place(hours, slots, block, slot):
+    free = TILE - TERMS * hours
+    return block * ((slots + free - 1) // free) + slot // free, TERMS * hours + slot % free
 
 
 def rounded(value):
@@ -42,7 +48,6 @@
     span = owned * w
     acts = blocks * slots * w
     values = acts + blocks * hours
-    lines = values + span
     row = lax.broadcasted_iota(jnp.int32, (campaigns, campaigns), 0)
     col = lax.broadcasted_iota(jnp.int32, (campaigns, campaigns), 1)
     source = lax.rem(row, span) // w * TILE + row // span * w + lax.rem(row, w)
@@ -59,20 +64,22 @@
     terms = [high, middle, price - high - middle, limit_high, limit - limit_high]
     terms.append(jnp.zeros((TILE - len(terms) * hours, campaigns), jnp.float32))
     terms = jnp.concatenate(terms, axis=0).astype(jnp.bfloat16)
-    terms = lax.dot_general(pick, terms, NT, preferred_element_type=jnp.float32).astype(jnp.bfloat16)
+    terms = lax.dot_general(pick, terms, NT, preferred_element_type=jnp.float32)
     loads[1].wait()
     loads[2].wait()
-    row = lax.broadcasted_iota(jnp.int32, (LINES, TILE), 0)
-    lane = lax.broadcasted_iota(jnp.int32, (LINES, TILE), 1)
-    entries = jnp.full((LINES, TILE), -TILE, jnp.int32)
+    row = lax.broadcasted_iota(jnp.int32, (span, TILE), 0)
+    lane = lax.broadcasted_iota(jnp.int32, (span, TILE), 1)
+    entries = jnp.full((span, TILE), -TILE, jnp.int32)
     for b in range(blocks):
         for k in range(slots):
-            here = jnp.logical_and(row == b, lane == k)
+            at_row, at_lane = entry_place(hours, slots, b, k)
+            here = jnp.logical_and(row == at_row, lane == at_lane)
             entries = jnp.where(here, jnp.where(k < counts[b], ids[b, 0, k] * w, -TILE), entries)
-    entries = entries.astype(jnp.float32).astype(jnp.bfloat16)
+    entries = jnp.concatenate([entries.astype(jnp.float32)] * devices, axis=0)
+    lane = lax.broadcasted_iota(jnp.int32, terms.shape, 1)
+    terms = jnp.where(lane < TERMS * hours, terms, entries).astype(jnp.bfloat16)
     for m in range(devices):
         out_ref[m, values : values + span, :] = terms[m * span : (m + 1) * span]
-        out_ref[m, lines : lines + LINES, :] = entries
     loads[5].wait()
     for b in range(blocks):
         own = act[:, b * TILE : (b + 1) * TILE]
@@ -95,17 +102,19 @@
     w = TILE // devices
     act_row = blocks * rows
     values = act_row + blocks * hours
-    lines = values + span
+    slots = rows // w
     terms = packets_ref[:, values : values + span, :].reshape(campaigns, TILE).astype(jnp.float32).T
-    terms = [terms[n * hours : (n + 1) * hours] for n in range(5)]
+    terms = [terms[n * hours : (n + 1) * hours] for n in range(TERMS)]
     anchor_ref[...] = terms[0] + terms[1] + terms[2]
     limit_ref[...] = terms[3] + terms[4]
     hour = lax.broadcasted_iota(jnp.int32, (ACT - hours, TILE), 0)
     tail = jnp.where(hour == 0, 1.0, 0.0).astype(jnp.bfloat16)
     padded = hot_ref.shape[1]
     row = lax.broadcasted_iota(jnp.int32, (padded, TILE), 0)
-    own_slot = lax.rem(row, rows) // w == lax.broadcasted_iota(jnp.int32, (padded, TILE), 1)
-    row_block = row // rows
+    lane = lax.broadcasted_iota(jnp.int32, (padded, TILE), 1)
+    at_row, at_lane = entry_place(hours, slots, row // rows, lax.rem(row, rows) // w)
+    at_row = jnp.where(lane == at_lane, at_row, -1)
+    lines = entry_place(hours, slots, blocks - 1, slots - 1)[0] + 1
     row = lax.broadcasted_iota(jnp.int32, (padded, campaigns), 0)
     wanted = lax.broadcasted_iota(jnp.int32, (padded, campaigns), 1) - lax.rem(row, w)
     wanted = jnp.where(row < blocks * rows, wanted, -2 * TILE).astype(jnp.float32)
@@ -115,11 +124,11 @@
     def _(step):
         for n in range(UNROLL):
             i = step * UNROLL + n
-            ids = packets_ref[i, lines : lines + LINES, :].astype(jnp.float32)
+            ids = packets_ref[i, values : values + span, :].astype(jnp.float32)
             spread = jnp.zeros((padded, TILE), jnp.float32)
+            for r in range(lines):
+                spread = jnp.where(at_row == r, ids[r : r + 1, :], spread)
             for b in range(blocks):
-                mine = jnp.logical_and(own_slot, row_block == b)
-                spread = jnp.where(mine, ids[b : b + 1, :], spread)
                 acts_ref[i, b * ACT : b * ACT + hours, :] = packets_ref[i, act_row + b * hours : act_row + (b + 1) * hours, :]
                 acts_ref[i, b * ACT + hours : (b + 1) * ACT, :] = tail
             first = jnp.dot(spread.astype(jnp.bfloat16), ones, preferred_element_type=jnp.float32)
@@ -138,7 +147,7 @@
     own = row // rows == lax.broadcasted_iota(jnp.int32, (listed, blocks * ACT), 1) // ACT
     block = lax.broadcasted_iota(jnp.int32, (ACT, padded), 1) // rows
     if listed < padded:
-        share_ref[:, listed:, :] = jnp.zeros((chunk, padded - listed, TILE), jnp.bfloat16)
+        share_ref[:, :, listed:] = jnp.zeros((chunk, TILE, padded - listed), jnp.bfloat16)
 
     def senders(step, total):
         first = step * chunk
@@ -149,9 +158,9 @@
         for n in range(chunk):
             part = jnp.dot(named_ref[n], acts_ref[first + n], preferred_element_type=jnp.float32)
             score = packets_ref[first + n, :listed, :].astype(jnp.float32)
-            share_ref[n, :listed, :] = jnp.clip(score + part, 0.0, 1.0).astype(jnp.bfloat16)
+            share_ref[n, :, :listed] = jnp.clip(score + part, 0.0, 1.0).astype(jnp.bfloat16).T
         for n in range(chunk):
-            each = lax.dot_general(acts_ref[first + n], share_ref[n], NT, preferred_element_type=jnp.float32)
+            each = jnp.dot(acts_ref[first + n], share_ref[n], preferred_element_type=jnp.float32)
             used = each[:ACT]
             for b in range(1, blocks):
                 used = jnp.where(block == b, each[b * ACT : (b + 1) * ACT], used)
@@ -271,7 +280,7 @@
     packets = kernel_call(
         cut_kernel,
         "cut",
-        shape((devices, blocks * (rows + hours) + span + LINES, TILE), bf16),
+        shape((devices, blocks * (rows + hours) + span, TILE), bf16),
         [HBM] * len(sources),
         VMEM,
         [
@@ -304,7 +313,7 @@
             [VMEM] * len(outs),
             [
                 pltpu.VMEM((chunk, blocks * rows, blocks * ACT), bf16),
-                pltpu.VMEM((chunk, padded, TILE), bf16),
+                pltpu.VMEM((chunk, TILE, padded), bf16),
                 pltpu.VMEM((2 * ACT, chunk * padded), bf16),
             ],
         )(*args)

time: 157 us -> 155 us (0.987)
  no operation moved by 1% of the time
where the time goes in v7:
time: 155 us
  blocking collectives  142 us (92%)
  Pallas kernels  11.6 us (7%)
    all_to_all x9, blocking collectives, swapped(): return lax.all_to_all(parts, axis, split_axis=0, concat_axis=0, tiled=True)  142 us
    pallas_call x4, Pallas kernels, direction(): kernel_call(functools.partial(direction_kernel, blocks, rows, entries, ki...  8.78 us

profile of v7, /device:TPU:1, one launch (start us, length us, event | category | flops | bytes accessed | tf_op | source)
XLA Modules:
  0.0 154.7 jit_solution(1344574502300448507)
XLA Ops:
  0.6 2.0 %cut.1 = bf16[32,152,128]{2,1,0:T(8,128)(2,1)S(1)} custom-call(bf16[2,1,12,128,128]{4,3,2,1,0:T(8,128)(2,1)} %scores_hbm.1, s32[2,1,12]{2,1,0:T(1,128)} %ids_hbm.1, s32[2]{0:T(128)} %bitcast.1, f32[24,256]{1,0:T(8,128)} %anchor_ref.1, f32[24,256]{1,0:T(8,128)} %limit_hbm.1, bf16[24,256]{1,0:T(8,128)(2,1)} %act_hbm.1), custom_call_target="tpu_custom_call" | custom-call | tf_op jit(solution)/shard_map/cut/pallas_call | solution.py:280
  2.6 29.1 %all_to_all.45.refs_0_ = bf16[32,152,128]{2,1,0:T(8,128)(2,1)S(1)} all-to-all(bf16[32,152,128]{2,1,0:T(8,128)(2,1)S(1)} %cut.1), channel_id=1, replica_groups=mesh['users_0'=4,'users_1'=4,'users_2'=2,'camps'=16] {'users_0','users_1..., dimensions={0} | all-to-all | bytes 2490368 | tf_op jit(solution)/shard_map/all_to_all | solution.py:250
  31.7 3.1 %direction.4 = (f32[24,256]{1,0:T(8,128)S(1)}, f32[32,1,128]{2,1,0:T(1,128)S(1)}, f32[24,256]{1,0:T(8,128)S(1)}, f32[24,256]{1,0:T(8,128)S(1)}, bf16[32,128,256]...) custom-call(bf16[32,152,128]{2,1,0:T(8,128)(2,1)S(1)} %all_to_all.45.refs_0_), custom_call_target="tpu_custom_call" | custom-call | tf_op jit(solution)/shard_map/direction/pallas_call | solution.py:308
  34.8 10.6 %all_to_all.46.parts_ref = f32[32,1,128]{2,1,0:T(1,128)S(1)} all-to-all(f32[32,1,128]{2,1,0:T(1,128)S(1)} %get-tuple-element.18), channel_id=1, replica_groups=mesh['users_0'=4,'users_1'=4,'users_2'=2,'camps'=16] {'users_0','users_1..., dimensions={0} | all-to-all | bytes 32768 | tf_op jit(solution)/shard_map/all_to_all | solution.py:250
  45.4 24.8 %all_to_all.47.refs_6_ = f32[16,1,128]{2,1,0:T(1,128)S(1)} all-to-all(f32[16,1,128]{2,1,0:T(1,128)S(1)} %fold.4), channel_id=1, replica_groups=mesh['users_0'=4,'users_1'=4,'users_2'=2,'camps'=16] {'camps'}, dimensions={0} | all-to-all | bytes 16384 | tf_op jit(solution)/shard_map/all_to_all | solution.py:250
  70.2 1.8 %direction.5 = (f32[24,256]{1,0:T(8,128)S(1)}, f32[32,1,128]{2,1,0:T(1,128)S(1)}) custom-call(bf16[32,152,128]{2,1,0:T(8,128)(2,1)S(1)} %all_to_all.45.refs_0_, f32[24,256]{1,0:T(8,128)S(1)} %get-tuple-element.13.refs_1_.refs_5_, f32[24,256]{1,0:T(8,128)S(1)} %get-tuple-element.14.refs_2_, bf16[32,128,256]{2,1,0:T(8,128)(2,1)S(1)} %get-tuple-element.15.refs_3_, ...), custom_call_target="tpu_custom_call" | custom-call | tf_op jit(solution)/shard_map/direction/pallas_call | solution.py:308
  72.1 12.1 %all_to_all.48.parts_ref = f32[32,1,128]{2,1,0:T(1,128)S(1)} all-to-all(f32[32,1,128]{2,1,0:T(1,128)S(1)} %get-tuple-element.20), channel_id=1, replica_groups=mesh['users_0'=4,'users_1'=4,'users_2'=2,'camps'=16] {'users_0','users_1..., dimensions={0} | all-to-all | bytes 32768 | tf_op jit(solution)/shard_map/all_to_all | solution.py:250
  84.2 13.8 %all_to_all.49.refs_7_ = f32[16,1,128]{2,1,0:T(1,128)S(1)} all-to-all(f32[16,1,128]{2,1,0:T(1,128)S(1)} %fold.5), channel_id=1, replica_groups=mesh['users_0'=4,'users_1'=4,'users_2'=2,'camps'=16] {'camps'}, dimensions={0} | all-to-all | bytes 16384 | tf_op jit(solution)/shard_map/all_to_all | solution.py:250
  98.1 1.8 %direction.6 = (f32[24,256]{1,0:T(8,128)S(1)}, f32[32,1,128]{2,1,0:T(1,128)S(1)}, f32[24,256]{1,0:T(8,128)S(1)}) custom-call(bf16[32,152,128]{2,1,0:T(8,128)(2,1)S(1)} %all_to_all.45.refs_0_, f32[24,256]{1,0:T(8,128)S(1)} %get-tuple-element.13.refs_1_.refs_5_, f32[24,256]{1,0:T(8,128)S(1)} %get-tuple-element.14.refs_2_, ...), custom_call_target="tpu_custom_call" | custom-call | tf_op jit(solution)/shard_map/direction/pallas_call | solution.py:308
  99.9 11.8 %all_to_all.50.parts_ref = f32[32,1,128]{2,1,0:T(1,128)S(1)} all-to-all(f32[32,1,128]{2,1,0:T(1,128)S(1)} %get-tuple-element.23), channel_id=1, replica_groups=mesh['users_0'=4,'users_1'=4,'users_2'=2,'camps'=16] {'users_0','users_1..., dimensions={0} | all-to-all | bytes 32768 | tf_op jit(solution)/shard_map/all_to_all | solution.py:250
  111.8 13.8 %all_to_all.51.refs_7_ = f32[16,1,128]{2,1,0:T(1,128)S(1)} all-to-all(f32[16,1,128]{2,1,0:T(1,128)S(1)} %fold.6), channel_id=1, replica_groups=mesh['users_0'=4,'users_1'=4,'users_2'=2,'camps'=16] {'camps'}, dimensions={0} | all-to-all | bytes 16384 | tf_op jit(solution)/shard_map/all_to_all | solution.py:250
  125.6 0.0 copy-start
  125.6 2.0 %direction.7 = f32[32,8,128]{2,1,0:T(8,128)S(1)} custom-call(bf16[32,152,128]{2,1,0:T(8,128)(2,1)S(1)} %all_to_all.45.refs_0_, f32[24,256]{1,0:T(8,128)S(1)} %get-tuple-element.13.refs_1_.refs_5_, f32[24,256]{1,0:T(8,128)S(1)} %get-tuple-element.14.refs_2_, bf16[32,128,256]{2,1,0:T(8,128)(2,1)S(1)} %get-tuple-element.15.refs_3_, ...), custom_call_target="tpu_custom_call" | custom-call | tf_op jit(solution)/shard_map/direction/pallas_call | solution.py:308
  127.6 12.5 %all_to_all.52.parts_ref = f32[32,8,128]{2,1,0:T(8,128)S(1)} all-to-all(f32[32,8,128]{2,1,0:T(8,128)S(1)} %direction.7), channel_id=1, replica_groups=mesh['users_0'=4,'users_1'=4,'users_2'=2,'camps'=16] {'users_0','users_1..., dimensions={0} | all-to-all | bytes 262144 | tf_op jit(solution)/shard_map/all_to_all | solution.py:250
  140.1 13.8 %all_to_all.53.sums_ref = f32[16,1,128]{2,1,0:T(1,128)S(1)} all-to-all(f32[16,1,128]{2,1,0:T(1,128)S(1)} %fold.7), channel_id=1, replica_groups=mesh['users_0'=4,'users_1'=4,'users_2'=2,'camps'=16] {'camps'}, dimensions={0} | all-to-all | bytes 16384 | tf_op jit(solution)/shard_map/all_to_all | solution.py:250
  154.0 0.0 copy-done
  154.0 0.7 final.1
  (4 shorter events, 0.1 us)
Async XLA Ops:
  125.6 28.3 %copy-start = (f32[24,256]{1,0:T(8,128)S(1)}, f32[24,256]{1,0:T(8,128)}, u32[]{:S(2)}) copy-start(f32[24,256]{1,0:T(8,128)} %anchor_ref.1) | copy-start | bytes 73732

commit v8 on v7

--- a/solution.py
+++ b/solution.py
@@ -16,7 +16,7 @@
 TERMS = 5
 ACT = 32
 CHUNK = 32
-UNROLL = 8
+UNROLL = 32
 SUM_LANE = 64
 
 VMEM = pl.BlockSpec(memory_space=pltpu.VMEM)
@@ -118,7 +118,7 @@
     row = lax.broadcasted_iota(jnp.int32, (padded, campaigns), 0)
     wanted = lax.broadcasted_iota(jnp.int32, (padded, campaigns), 1) - lax.rem(row, w)
     wanted = jnp.where(row < blocks * rows, wanted, -2 * TILE).astype(jnp.float32)
-    ones = jnp.ones((TILE, campaigns), jnp.bfloat16)
+    ones = jnp.ones((TILE, TILE), jnp.bfloat16)
 
     @pl.loop(0, devices // UNROLL)
     def _(step):
@@ -132,6 +132,7 @@
                 acts_ref[i, b * ACT : b * ACT + hours, :] = packets_ref[i, act_row + b * hours : act_row + (b + 1) * hours, :]
                 acts_ref[i, b * ACT + hours : (b + 1) * ACT, :] = tail
             first = jnp.dot(spread.astype(jnp.bfloat16), ones, preferred_element_type=jnp.float32)
+            first = jnp.concatenate([first] * (campaigns // TILE), axis=1)
             hot_ref[i] = jnp.where(first == wanted, 1.0, 0.0).astype(jnp.bfloat16)
 
 

time: 155 us -> 155 us (level)
  no operation moved by 1% of the time
where the time goes in v8:
time: 155 us; the launch traced here: 154 us
  blocking collectives  142 us (92%)
  Pallas kernels  11 us (7%)
    all_to_all x9, blocking collectives, swapped(): return lax.all_to_all(parts, axis, split_axis=0, concat_axis=0, tiled=True)  142 us
    pallas_call x4, Pallas kernels, direction(): kernel_call(functools.partial(direction_kernel, blocks, rows, entries, ki...  8.18 us

profile of v8, /device:TPU:1, one launch (start us, length us, event | category | flops | bytes accessed | tf_op | source)
XLA Modules:
  0.0 154.1 jit_solution(15068524358712551555)
XLA Ops:
  0.6 2.0 %cut.1 = bf16[32,152,128]{2,1,0:T(8,128)(2,1)S(1)} custom-call(bf16[2,1,12,128,128]{4,3,2,1,0:T(8,128)(2,1)} %scores_hbm.1, s32[2,1,12]{2,1,0:T(1,128)} %ids_hbm.1, s32[2]{0:T(128)} %bitcast.1, f32[24,256]{1,0:T(8,128)} %anchor_ref.1, f32[24,256]{1,0:T(8,128)} %limit_hbm.1, bf16[24,256]{1,0:T(8,128)(2,1)} %act_hbm.1), custom_call_target="tpu_custom_call" | custom-call | tf_op jit(solution)/shard_map/cut/pallas_call | solution.py:281
  2.6 29.1 %all_to_all.45.refs_0_ = bf16[32,152,128]{2,1,0:T(8,128)(2,1)S(1)} all-to-all(bf16[32,152,128]{2,1,0:T(8,128)(2,1)S(1)} %cut.1), channel_id=1, replica_groups=mesh['users_0'=4,'users_1'=4,'users_2'=2,'camps'=16] {'users_0','users_1..., dimensions={0} | all-to-all | bytes 2490368 | tf_op jit(solution)/shard_map/all_to_all | solution.py:251
  31.7 2.5 %direction.4 = (f32[24,256]{1,0:T(8,128)S(1)}, f32[32,1,128]{2,1,0:T(1,128)S(1)}, f32[24,256]{1,0:T(8,128)S(1)}, f32[24,256]{1,0:T(8,128)S(1)}, bf16[32,128,256]...) custom-call(bf16[32,152,128]{2,1,0:T(8,128)(2,1)S(1)} %all_to_all.45.refs_0_), custom_call_target="tpu_custom_call" | custom-call | tf_op jit(solution)/shard_map/direction/pallas_call | solution.py:309
  34.2 10.6 %all_to_all.46.parts_ref = f32[32,1,128]{2,1,0:T(1,128)S(1)} all-to-all(f32[32,1,128]{2,1,0:T(1,128)S(1)} %get-tuple-element.18), channel_id=1, replica_groups=mesh['users_0'=4,'users_1'=4,'users_2'=2,'camps'=16] {'users_0','users_1..., dimensions={0} | all-to-all | bytes 32768 | tf_op jit(solution)/shard_map/all_to_all | solution.py:251
  44.8 24.8 %all_to_all.47.refs_6_ = f32[16,1,128]{2,1,0:T(1,128)S(1)} all-to-all(f32[16,1,128]{2,1,0:T(1,128)S(1)} %fold.4), channel_id=1, replica_groups=mesh['users_0'=4,'users_1'=4,'users_2'=2,'camps'=16] {'camps'}, dimensions={0} | all-to-all | bytes 16384 | tf_op jit(solution)/shard_map/all_to_all | solution.py:251
  69.6 1.8 %direction.5 = (f32[24,256]{1,0:T(8,128)S(1)}, f32[32,1,128]{2,1,0:T(1,128)S(1)}) custom-call(bf16[32,152,128]{2,1,0:T(8,128)(2,1)S(1)} %all_to_all.45.refs_0_, f32[24,256]{1,0:T(8,128)S(1)} %get-tuple-element.13.refs_1_.refs_5_, f32[24,256]{1,0:T(8,128)S(1)} %get-tuple-element.14.refs_2_, bf16[32,128,256]{2,1,0:T(8,128)(2,1)S(1)} %get-tuple-element.15.refs_3_, ...), custom_call_target="tpu_custom_call" | custom-call | tf_op jit(solution)/shard_map/direction/pallas_call | solution.py:309
  71.5 12.1 %all_to_all.48.parts_ref = f32[32,1,128]{2,1,0:T(1,128)S(1)} all-to-all(f32[32,1,128]{2,1,0:T(1,128)S(1)} %get-tuple-element.20), channel_id=1, replica_groups=mesh['users_0'=4,'users_1'=4,'users_2'=2,'camps'=16] {'users_0','users_1..., dimensions={0} | all-to-all | bytes 32768 | tf_op jit(solution)/shard_map/all_to_all | solution.py:251
  83.6 13.8 %all_to_all.49.refs_7_ = f32[16,1,128]{2,1,0:T(1,128)S(1)} all-to-all(f32[16,1,128]{2,1,0:T(1,128)S(1)} %fold.5), channel_id=1, replica_groups=mesh['users_0'=4,'users_1'=4,'users_2'=2,'camps'=16] {'camps'}, dimensions={0} | all-to-all | bytes 16384 | tf_op jit(solution)/shard_map/all_to_all | solution.py:251
  97.4 1.8 %direction.6 = (f32[24,256]{1,0:T(8,128)S(1)}, f32[32,1,128]{2,1,0:T(1,128)S(1)}, f32[24,256]{1,0:T(8,128)S(1)}) custom-call(bf16[32,152,128]{2,1,0:T(8,128)(2,1)S(1)} %all_to_all.45.refs_0_, f32[24,256]{1,0:T(8,128)S(1)} %get-tuple-element.13.refs_1_.refs_5_, f32[24,256]{1,0:T(8,128)S(1)} %get-tuple-element.14.refs_2_, ...), custom_call_target="tpu_custom_call" | custom-call | tf_op jit(solution)/shard_map/direction/pallas_call | solution.py:309
  99.3 11.8 %all_to_all.50.parts_ref = f32[32,1,128]{2,1,0:T(1,128)S(1)} all-to-all(f32[32,1,128]{2,1,0:T(1,128)S(1)} %get-tuple-element.23), channel_id=1, replica_groups=mesh['users_0'=4,'users_1'=4,'users_2'=2,'camps'=16] {'users_0','users_1..., dimensions={0} | all-to-all | bytes 32768 | tf_op jit(solution)/shard_map/all_to_all | solution.py:251
  111.2 13.8 %all_to_all.51.refs_7_ = f32[16,1,128]{2,1,0:T(1,128)S(1)} all-to-all(f32[16,1,128]{2,1,0:T(1,128)S(1)} %fold.6), channel_id=1, replica_groups=mesh['users_0'=4,'users_1'=4,'users_2'=2,'camps'=16] {'camps'}, dimensions={0} | all-to-all | bytes 16384 | tf_op jit(solution)/shard_map/all_to_all | solution.py:251
  125.0 0.0 copy-start
  125.0 2.0 %direction.7 = f32[32,8,128]{2,1,0:T(8,128)S(1)} custom-call(bf16[32,152,128]{2,1,0:T(8,128)(2,1)S(1)} %all_to_all.45.refs_0_, f32[24,256]{1,0:T(8,128)S(1)} %get-tuple-element.13.refs_1_.refs_5_, f32[24,256]{1,0:T(8,128)S(1)} %get-tuple-element.14.refs_2_, bf16[32,128,256]{2,1,0:T(8,128)(2,1)S(1)} %get-tuple-element.15.refs_3_, ...), custom_call_target="tpu_custom_call" | custom-call | tf_op jit(solution)/shard_map/direction/pallas_call | solution.py:309
  127.0 12.5 %all_to_all.52.parts_ref = f32[32,8,128]{2,1,0:T(8,128)S(1)} all-to-all(f32[32,8,128]{2,1,0:T(8,128)S(1)} %direction.7), channel_id=1, replica_groups=mesh['users_0'=4,'users_1'=4,'users_2'=2,'camps'=16] {'users_0','users_1..., dimensions={0} | all-to-all | bytes 262144 | tf_op jit(solution)/shard_map/all_to_all | solution.py:251
  139.5 13.8 %all_to_all.53.sums_ref = f32[16,1,128]{2,1,0:T(1,128)S(1)} all-to-all(f32[16,1,128]{2,1,0:T(1,128)S(1)} %fold.7), channel_id=1, replica_groups=mesh['users_0'=4,'users_1'=4,'users_2'=2,'camps'=16] {'camps'}, dimensions={0} | all-to-all | bytes 16384 | tf_op jit(solution)/shard_map/all_to_all | solution.py:251
  153.3 0.0 copy-done
  153.4 0.7 final.1
  (4 shorter events, 0.1 us)
Async XLA Ops:
  125.0 28.3 %copy-start = (f32[24,256]{1,0:T(8,128)S(1)}, f32[24,256]{1,0:T(8,128)}, u32[]{:S(2)}) copy-start(f32[24,256]{1,0:T(8,128)} %anchor_ref.1) | copy-start | bytes 73732
